TPU v7x, 32 devices: a whole 2x2x4 slice. The times are simulated.
32 devices in a mesh: expert: 8 (over z, x), dp: 4 (over y, core).
Axes of the slice: x: 2, y: 2, z: 4, core: 2. Of those that a mesh axis runs over, the one named last changes fastest.
Arguments:
- tokens: bfloat16 [1024, 4096], P('expert', 'dp'), may hold values from -6 to 6
- out_grad: bfloat16 [1024, 4096], P('expert', 'dp'), may hold values from -6 to 6
- routes: int32 [1024, 4], P('expert'), may hold values from 0 to 7, all different within a row; in each aligned block of 128 rows (0 to 127, 128 to 255, ...) at most 72 rows name the same one
- gate_weights: float32 [1024, 4], P('expert'), may hold values from 0.05 to 0.5
- previous_home: int32 [8], replicated, may hold values from 0 to 7, each once
- next_home: int32 [8], replicated, may hold values from 0 to 7, each once
- w_in: bfloat16 [8, 2, 4096, 1024], P('expert', None, None, 'dp'), may hold values from -0.09375 to 0.09375
- w_out: bfloat16 [8, 1024, 4096], P('expert', 'dp'), may hold values from -0.1875 to 0.1875
- first_moment: float32 [8, 1024, 4096], P('expert', 'dp'), may hold values from -12 to 12
- second_moment: float32 [8, 1024, 4096], P('expert', 'dp'), may hold values from 1 to 30
Outputs:
- token_grad: bfloat16 [1024, 4096], P('expert', 'dp')
- new_first: float32 [8, 1024, 4096], P('expert', 'dp')
- new_second: float32 [8, 1024, 4096], P('expert', 'dp')
- adam_step: bfloat16 [8, 1024, 4096], P('expert', 'dp')
Inputs may be any that keep to these rules, and one draw needn't show every extreme that they name: `routes`: in each device's block of 128 tokens at most 72 pairs name the same expert, and some block reaches 72. `previous_home`: each expert appears once. `next_home`: each expert appears once.
All inputs are finite; a program needn't handle non-finite values.
Results may differ from a plain program's by a relative error of at most 0.0064.
Values may be sent and summed in bfloat16 or wider, within the bound.
No kernel may reach another device: no remote copies, remote signals or barrier semaphores. Data moves between devices by JAX's collectives and lax.ppermute only.
A program may use at most 128 MiB of HBM per device.

v0:
```python
import jax
import jax.numpy as jnp
from jax import lax
from jax.experimental import pallas as pl
from jax.experimental.pallas import tpu as pltpu
from jax.sharding import PartitionSpec as P


beta_one = 0.9
beta_two = 0.95
epsilon = 1e-08


def swap(value, axis, mask):
    size = lax.axis_size(axis)
    return lax.ppermute(value, axis, [(j, j ^ mask) for j in range(size)])


def gather_parts(value, axis):
    parts = {0: value}
    mask = lax.axis_size(axis) // 2
    while mask:
        parts.update({k ^ mask: swap(v, axis, mask) for k, v in list(parts.items())})
        mask //= 2
    return [parts[k] for k in range(len(parts))]


def scatter_sum(parts, axis):
    parts = dict(enumerate(parts))
    mask = 1
    while len(parts) > 1:
        kept = {}
        for k in [k for k in parts if not k & mask]:
            other = swap(parts[k ^ mask].astype(jnp.bfloat16), axis, mask)
            kept[k] = parts[k].astype(jnp.float32) + other.astype(jnp.float32)
        parts = kept
        mask *= 2
    return parts[0]


def finish_body(lane_ref, grad_ref, first_ref, second_ref, out_first, out_second, out_step):
    weight_grad = grad_ref[0]
    new_first = beta_one * first_ref[...].astype(jnp.float32) + (1.0 - beta_one) * weight_grad
    scaled = (1.0 - beta_two) * weight_grad * weight_grad
    new_second = beta_two * second_ref[...].astype(jnp.float32) + scaled
    out_first[...] = new_first
    out_second[...] = new_second
    out_step[...] = (new_first / (jnp.sqrt(new_second) + epsilon)).astype(jnp.bfloat16)


def finish(lane, weight_grad, first, second):
    ways, hidden, columns = weight_grad.shape
    rows = max(hidden // 4, 16)
    wide = pl.BlockSpec((rows, columns), lambda k, i, lane: (i, lane[0] ^ k))
    shape = (hidden, ways * columns)
    return pl.pallas_call(
        finish_body,
        out_shape=(
            jax.ShapeDtypeStruct(shape, jnp.float32),
            jax.ShapeDtypeStruct(shape, jnp.float32),
            jax.ShapeDtypeStruct(shape, jnp.bfloat16),
        ),
        grid_spec=pltpu.PrefetchScalarGridSpec(
            num_scalar_prefetch=1,
            grid=(ways, hidden // rows),
            in_specs=[
                pl.BlockSpec((1, rows, columns), lambda k, i, lane: (k, i, 0)),
                wide,
                wide,
            ],
            out_specs=(wide, wide, wide),
        ),
        name="finish",
    )(lane.reshape(1), weight_grad, first, second)


def spread(value):
    return lax.all_to_all(value, "expert", split_axis=0, concat_axis=0, tiled=True)


def dot(left, right, dims):
    return lax.dot_general(left, right, (dims, ((), ())), preferred_element_type=jnp.float32)


def per_device(
    tokens,
    out_grad,
    routes,
    gate_weights,
    previous_home,
    next_home,
    w_in,
    w_out,
    first_moment,
    second_moment,
):
    devices = lax.axis_size("expert")
    ways = lax.axis_size("dp")
    half = devices // 2
    tok_count, top_count = routes.shape
    experts = previous_home.shape[0]
    capacity = tok_count * top_count * 9 // (8 * experts)
    slots = devices * capacity
    columns = tokens.shape[1]
    hidden = w_out.shape[1]
    place = lax.axis_index("expert")
    side = place // half
    lane = lax.axis_index("dp")
    spot = (place % half) ^ jnp.arange(half, dtype=jnp.int32)

    homes = jnp.arange(devices, dtype=jnp.int32)
    matched = (next_home[:, None] == homes[None, :]).astype(jnp.int32)
    source = jnp.sum(matched * previous_home[:, None], axis=0)

    def relocate(value):
        rows = value.shape[0] // devices
        pieces = spread(value.reshape(devices, rows, value.shape[1]))
        pieces = jnp.take(pieces, source, axis=0)
        return spread(pieces).reshape(value.shape)

    def across_half(blocks):
        moved = [blocks[r] if r == 0 else swap(blocks[r], "expert", r) for r in range(half)]
        return jnp.concatenate(moved, axis=0)

    far_tokens = swap(tokens, "expert", half)
    far_routes = swap(routes, "expert", half)
    far_gates = swap(gate_weights, "expert", half)
    far_grads = swap(out_grad, "expert", half)

    old_first = relocate(first_moment[0].astype(jnp.bfloat16))
    old_second = relocate(second_moment[0].astype(jnp.bfloat16))

    both_routes = jnp.stack([routes, far_routes])
    both_gates = jnp.stack([gate_weights, far_gates])
    both_tokens = jnp.concatenate([tokens, far_tokens], axis=0)
    both_grads = jnp.concatenate([out_grad, far_grads], axis=0)
    block_side = jnp.stack([side, 1 - side]).astype(jnp.float32)
    earlier = jnp.tril(jnp.ones((tok_count, tok_count), jnp.bfloat16), -1)
    own_homes = place ^ jnp.arange(half, dtype=jnp.int32)

    def selection(home_table):
        chosen = (home_table[None, :] == own_homes[:, None]).astype(jnp.int32)
        expert_of = jnp.sum(chosen * jnp.arange(experts, dtype=jnp.int32)[None, :], axis=1)
        hit = both_routes[:, None, :, :] == expert_of[None, :, None, None]
        member = jnp.any(hit, axis=3)
        gate = jnp.sum(jnp.where(hit, both_gates[:, None, :, :], 0.0), axis=3)
        before = dot(member.astype(jnp.bfloat16), earlier, (((2,), (1,))))
        slot = jnp.where(member, before + block_side[:, None, None] * capacity, -1.0)
        slot = jnp.concatenate([slot[0], slot[1]], axis=1)
        gate = jnp.concatenate([gate[0], gate[1]], axis=1)
        numbers = lax.broadcasted_iota(jnp.int32, (half, 2 * capacity, 2 * tok_count), 1)
        picks = numbers == slot.astype(jnp.int32)[:, None, :]
        slot_gate = jnp.sum(jnp.where(picks, gate[:, None, :], 0.0), axis=2)
        picks = picks.astype(jnp.bfloat16).reshape(slots, 2 * tok_count)
        return picks, slot_gate.reshape(slots, 1)

    picks_now, gate_now = selection(previous_home)
    picks_next, gate_next = selection(next_home)

    def send(rows):
        rows = rows.astype(jnp.bfloat16).reshape(half, 2 * capacity, columns)
        return across_half(rows)

    plain = ((1,), (0,))

    def deliver(rows):
        rows = send(rows)
        return gather_parts(rows, "dp")

    rows_parts = deliver(dot(picks_now, both_tokens, plain))
    grad_parts = deliver(dot(picks_now, both_grads, plain) * gate_now)
    next_parts = deliver(dot(picks_next, both_grads, plain) * gate_next)

    order = lane ^ jnp.arange(ways, dtype=jnp.int32)
    weight_in = jnp.concatenate([w_in[0, 0], w_in[0, 1]], axis=1).reshape(ways, columns, 2 * hidden)
    weight_out = w_out[0].reshape(hidden, ways, columns)
    weight_in = [lax.dynamic_index_in_dim(weight_in, order[k], 0, False) for k in range(ways)]
    weight_out = [lax.dynamic_index_in_dim(weight_out, order[k], 1, False) for k in range(ways)]

    pre = sum(dot(rows_parts[k], weight_in[k], plain) for k in range(ways))
    gate_pre, up_value = pre[:, :hidden], pre[:, hidden:]
    sigmoid_gate = jax.nn.sigmoid(gate_pre)
    silu_gate = gate_pre * sigmoid_gate
    activation = (silu_gate * up_value).astype(jnp.bfloat16).reshape(half, 2 * capacity, hidden)
    activation = jnp.take(activation, spot, axis=0).reshape(slots, hidden)
    activation = relocate(activation)
    activation = jnp.take(activation.reshape(half, 2 * capacity, hidden), spot, axis=0)
    activation = activation.reshape(slots, hidden)
    act_grad = sum(dot(grad_parts[k], weight_out[k], ((1,), (1,))) for k in range(ways))
    gate_grad = act_grad * up_value * sigmoid_gate * (1.0 + gate_pre * (1.0 - sigmoid_gate))
    up_grad = act_grad * silu_gate
    both_grad = jnp.concatenate([gate_grad, up_grad], axis=1).astype(jnp.bfloat16)
    pieces = [dot(both_grad, weight_in[k], ((1,), (1,))).astype(jnp.bfloat16) for k in range(ways)]
    summed = scatter_sum(pieces, "dp").astype(jnp.bfloat16)
    returned = across_half(summed.reshape(half, 2 * capacity, columns))
    token_sums = dot(picks_now, returned, ((0,), (0,)))
    far_sums = swap(token_sums[tok_count:].astype(jnp.bfloat16), "expert", half)
    token_grad = (token_sums[:tok_count] + far_sums.astype(jnp.float32)).astype(jnp.bfloat16)

    weight_grad = jnp.stack([dot(activation, part, ((0,), (0,))) for part in next_parts])
    new_first, new_second, adam_step = finish(lane, weight_grad, old_first, old_second)
    return (token_grad, new_first[None], new_second[None], adam_step[None])


def solution(mesh):
    return jax.shard_map(
        per_device,
        mesh=mesh,
        in_specs=(
            P("expert", "dp"),
            P("expert", "dp"),
            P("expert", None),
            P("expert", None),
            P(),
            P(),
            P("expert", None, None, "dp"),
            P("expert", "dp", None),
            P("expert", "dp", None),
            P("expert", "dp", None),
        ),
        out_specs=(
            P("expert", "dp"),
            P("expert", "dp", None),
            P("expert", "dp", None),
            P("expert", "dp", None),
        ),
        check_vma=False,
    )
```

profile of v0, /device:TPU:0, one launch (start us, length us, event | category | flops | bytes accessed | tf_op | source)
XLA Modules:
  0.0 414.7 jit_solution(5424685646772484297)
XLA Ops:
  0.6 4.1 collective-permute-start
  11.1 19.5 %collective-permute-done.2 = f32[128,4]{0,1:T(4,128)S(1)} collective-permute-done((f32[128,4]{0,1:T(4,128)}, f32[128,4]{0,1:T(4,128)S(1)}, u32[]{:S(2)}, u32[]{:S(2)}) %collective-permute-start.2) | collective-permute-done | bytes 2080 | tf_op jit(solution)/shard_map/ppermute | solution.py:16
  45.9 4.9 %collective-permute-done.11 = bf16[144,1024]{1,0:T(8,128)(2,1)S(1)} collective-permute-done((bf16[144,1024]{1,0:T(8,128)(2,1)S(1)}, bf16[144,1024]{1,0:T(8,128)(2,1)S(1)}, u32[]{:S(2)}, u32[]{:S(2)}) %collective-permute-start.11) | collective-permute-done | bytes 294944 | tf_op jit(solution)/shard_map/ppermute | solution.py:16
  57.1 4.4 %collective-permute-done.4 = bf16[144,1024]{1,0:T(8,128)(2,1)S(1)} collective-permute-done((bf16[144,1024]{1,0:T(8,128)(2,1)S(1)}, bf16[144,1024]{1,0:T(8,128)(2,1)S(1)}, u32[]{:S(2)}, u32[]{:S(2)}) %collective-permute-start.4) | collective-permute-done | bytes 294944 | tf_op jit(solution)/shard_map/ppermute | solution.py:16
  71.8 4.1 copy.25
  81.0 24.1 %collective-permute-done.7 = bf16[576,1024]{1,0:T(8,128)(2,1)} collective-permute-done((bf16[576,1024]{1,0:T(8,128)(2,1)}, bf16[576,1024]{1,0:T(8,128)(2,1)}, u32[]{:S(2)}, u32[]{:S(2)}) %collective-permute-start.7) | collective-permute-done | bytes 1179680 | tf_op jit(solution)/shard_map/ppermute | solution.py:16
  121.5 4.1 all-to-all-start
  125.6 3.8 convert_element_type.117
  129.4 6.7 %all-to-all-done = bf16[8,72,256]{2,1,0:T(8,128)(2,1)} async-done(((bf16[8,72,256]{2,1,0:T(8,128)(2,1)}), bf16[8,72,256]{2,1,0:T(8,128)(2,1)}, u32[]{:S(2)}, u32[]{:S(2)}) %all-to-all-start) | async-done | bytes 294944 | tf_op jit(solution)/shard_map/all_to_all | solution.py:78
  136.1 4.4 %all-to-all-start.4 = ((bf16[8,32,4096]{2,1,0:T(8,128)(2,1)}), bf16[8,32,4096]{2,1,0:T(8,128)(2,1)}, u32[]{:S(2)}, u32[]{:S(2)}) async-start(bf16[8,32,4096]{2,1,0:T(8,128)(2,1)} %bitcast.133), calls=%async_computation.4 | async-start | bytes 4194304 | tf_op jit(solution)/shard_map/all_to_all | solution.py:78
  140.5 3.8 convert_element_type.115
  144.3 44.5 %all-to-all-done.4 = bf16[8,32,4096]{2,1,0:T(8,128)(2,1)} async-done(((bf16[8,32,4096]{2,1,0:T(8,128)(2,1)}), bf16[8,32,4096]{2,1,0:T(8,128)(2,1)}, u32[]{:S(2)}, u32[]{:S(2)}) %all-to-all-start.4) | async-done | bytes 2097184 | tf_op jit(solution)/shard_map/all_to_all | solution.py:78
  188.8 4.5 %all-to-all-start.2 = ((bf16[8,32,4096]{2,1,0:T(8,128)(2,1)}), bf16[8,32,4096]{2,1,0:T(8,128)(2,1)}, u32[]{:S(2)}, u32[]{:S(2)}) async-start(bf16[8,32,4096]{2,1,0:T(8,128)(2,1)} %bitcast.132), calls=%async_computation.2 | async-start | bytes 4194304 | tf_op jit(solution)/shard_map/all_to_all | solution.py:78
  201.1 40.0 %all-to-all-done.2 = bf16[8,32,4096]{2,1,0:T(8,128)(2,1)} async-done(((bf16[8,32,4096]{2,1,0:T(8,128)(2,1)}), bf16[8,32,4096]{2,1,0:T(8,128)(2,1)}, u32[]{:S(2)}, u32[]{:S(2)}) %all-to-all-start.2) | async-done | bytes 2097184 | tf_op jit(solution)/shard_map/all_to_all | solution.py:78
  241.1 4.1 all-to-all-start.1
  248.8 4.7 %broadcast_select_fusion = (bf16[8,32,4096]{2,1,0:T(8,128)(2,1)}, bf16[8,32,4096]{2,1,0:T(8,128)(2,1)}) fusion(bf16[8,32,4096]{2,1,0:T(8,128)(2,1)} %gather_fusion.4, pred[8]{0:T(512)(128)(4,1)S(1)} %compare_and_fusion.1, bf16[8,32,4096]{2,1,0:T(8,128)(2,1)} %gather_fusion.3), kind=kLoop, calls=%fused_computation.18 | loop fusion | flops 2097152 | bytes 8388616 | tf_op jit(solution)/shard_map/jit(_take)/select_n | solution.py:118
  254.6 4.7 %all-to-all-start.3 = ((bf16[8,32,4096]{2,1,0:T(8,128)(2,1)}), bf16[8,32,4096]{2,1,0:T(8,128)(2,1)}, u32[]{:S(2)}, u32[]{:S(2)}) async-start(bf16[8,32,4096]{2,1,0:T(8,128)(2,1)} %get-tuple-element.50), calls=%async_computation.3 | async-start | bytes 4194304 | tf_op jit(solution)/shard_map/all_to_all | solution.py:78
  267.5 39.6 %all-to-all-done.3 = bf16[8,32,4096]{2,1,0:T(8,128)(2,1)} async-done(((bf16[8,32,4096]{2,1,0:T(8,128)(2,1)}), bf16[8,32,4096]{2,1,0:T(8,128)(2,1)}, u32[]{:S(2)}, u32[]{:S(2)}) %all-to-all-start.3) | async-done | bytes 2097184 | tf_op jit(solution)/shard_map/all_to_all | solution.py:78
  307.0 5.7 %all-to-all-start.5 = ((bf16[8,32,4096]{2,1,0:T(8,128)(2,1)}), bf16[8,32,4096]{2,1,0:T(8,128)(2,1)}, u32[]{:S(2)}, u32[]{:S(2)}) async-start(bf16[8,32,4096]{2,1,0:T(8,128)(2,1)} %get-tuple-element.49), calls=%async_computation.5 | async-start | bytes 4194304 | tf_op jit(solution)/shard_map/all_to_all | solution.py:78
  322.4 22.0 %collective-permute-done.27 = bf16[576,1024]{1,0:T(8,128)(2,1)} collective-permute-done((bf16[576,1024]{1,0:T(8,128)(2,1)}, bf16[576,1024]{1,0:T(8,128)(2,1)}, u32[]{:S(2)}, u32[]{:S(2)}) %collective-permute-start.27) | collective-permute-done | bytes 1179680 | tf_op jit(solution)/shard_map/ppermute | solution.py:16
  349.8 18.6 %collective-permute-done.18 = bf16[576,1024]{1,0:T(8,128)(2,1)} collective-permute-done((bf16[576,1024]{1,0:T(8,128)(2,1)}, bf16[576,1024]{1,0:T(8,128)(2,1)}, u32[]{:S(2)}, u32[]{:S(2)}) %collective-permute-start.18) | collective-permute-done | bytes 1179680 | tf_op jit(solution)/shard_map/ppermute | solution.py:16
  381.7 4.2 %collective-permute-done.20 = bf16[144,1024]{1,0:T(8,128)(2,1)S(1)} collective-permute-done((bf16[144,1024]{1,0:T(8,128)(2,1)S(1)}, bf16[144,1024]{1,0:T(8,128)(2,1)S(1)}, u32[]{:S(2)}, u32[]{:S(2)}) %collective-permute-start.20) | collective-permute-done | bytes 294944 | tf_op jit(solution)/shard_map/ppermute | solution.py:16
  393.2 8.1 %collective-permute-done.22 = bf16[128,1024]{1,0:T(8,128)(2,1)S(1)} collective-permute-done((bf16[128,1024]{1,0:T(8,128)(2,1)S(1)}, bf16[128,1024]{1,0:T(8,128)(2,1)S(1)}, u32[]{:S(2)}, u32[]{:S(2)}) %collective-permute-start.22) | collective-permute-done | bytes 262176 | tf_op jit(solution)/shard_map/ppermute | solution.py:16
  402.2 12.5 %finish.1 = (f32[256,4096]{1,0:T(8,128)}, f32[256,4096]{1,0:T(8,128)}, bf16[256,4096]{1,0:T(8,128)(2,1)}) custom-call(s32[1]{0:T(128)} %bitcast.27.lane_ref, f32[4,256,1024]{2,1,0:T(8,128)} %pad_maximum_fusion.grad_ref, bf16[256,4096]{1,0:T(8,128)(2,1)} %bitcast.44.first_ref, bf16[256,4096]{1,0:T(8,128)(2,1)} %bitcast.46.second_ref), custom_call_target="tpu_custom_call" | custom-call | tf_op jit(solution)/shard_map/finish/pallas_call | solution.py:56
  (165 shorter events, 108.6 us)
Async XLA Ops:
  4.8 27.2 %collective-permute-start.9 = (bf16[128,1024]{1,0:T(8,128)(2,1)}, bf16[128,1024]{1,0:T(8,128)(2,1)S(1)}, u32[]{:S(2)}, u32[]{:S(2)}) collective-permute-start(bf16[128,1024]{1,0:T(8,128)(2,1)} %param.14), channel_id=1, source_target_pairs={{0,16},{4,20},{8,24},{12,28},{16,0},{20,4},{24,8},{28,12},{1,17},{... | collective-permute-start | bytes 786440 | tf_op jit(solution)/shard_map/ppermute | solution.py:16
  4.8 32.2 %collective-permute-start.1 = (bf16[128,1024]{1,0:T(8,128)(2,1)}, bf16[128,1024]{1,0:T(8,128)(2,1)S(1)}, u32[]{:S(2)}, u32[]{:S(2)}) collective-permute-start(bf16[128,1024]{1,0:T(8,128)(2,1)} %param.15), channel_id=1, source_target_pairs={{0,16},{4,20},{8,24},{12,28},{16,0},{20,4},{24,8},{28,12},{1,17},{... | collective-permute-start | bytes 786440 | tf_op jit(solution)/shard_map/ppermute | solution.py:16
  7.7 22.9 %collective-permute-start.2 = (f32[128,4]{0,1:T(4,128)}, f32[128,4]{0,1:T(4,128)S(1)}, u32[]{:S(2)}, u32[]{:S(2)}) collective-permute-start(f32[128,4]{0,1:T(4,128)} %param.17), channel_id=1, source_target_pairs={{0,16},{4,20},{8,24},{12,28},{16,0},{20,4},{24,8},{28,12},{1,17},{... | collective-permute-start | bytes 6152 | tf_op jit(solution)/shard_map/ppermute | solution.py:16
  33.6 17.2 %collective-permute-start.11 = (bf16[144,1024]{1,0:T(8,128)(2,1)S(1)}, bf16[144,1024]{1,0:T(8,128)(2,1)S(1)}, u32[]{:S(2)}, u32[]{:S(2)}) collective-permute-start(bf16[144,1024]{1,0:T(8,128)(2,1)S(1)} %get-tuple-element.33), channel_id=1, source_target_pairs={{0,8},{4,12},{8,0},{12,4},{16,24},{20,28},{24,16},{28,20},{1,9},{5... | collective-permute-start | bytes 884744 | tf_op jit(solution)/shard_map/ppermute | solution.py:16
  37.6 19.4 %collective-permute-start.5 = (bf16[144,1024]{1,0:T(8,128)(2,1)S(1)}, bf16[144,1024]{1,0:T(8,128)(2,1)S(1)}, u32[]{:S(2)}, u32[]{:S(2)}) collective-permute-start(bf16[144,1024]{1,0:T(8,128)(2,1)S(1)} %get-tuple-element.36), channel_id=1, source_target_pairs={{0,12},{4,8},{8,4},{12,0},{16,28},{20,24},{24,20},{28,16},{1,13},{... | collective-permute-start | bytes 884744 | tf_op jit(solution)/shard_map/ppermute | solution.py:16
  38.6 22.8 %collective-permute-start.4 = (bf16[144,1024]{1,0:T(8,128)(2,1)S(1)}, bf16[144,1024]{1,0:T(8,128)(2,1)S(1)}, u32[]{:S(2)}, u32[]{:S(2)}) collective-permute-start(bf16[144,1024]{1,0:T(8,128)(2,1)S(1)} %get-tuple-element.37), channel_id=1, source_target_pairs={{0,8},{4,12},{8,0},{12,4},{16,24},{20,28},{24,16},{28,20},{1,9},{5... | collective-permute-start | bytes 884744 | tf_op jit(solution)/shard_map/ppermute | solution.py:16
  51.9 29.2 %collective-permute-start.14 = (bf16[576,1024]{1,0:T(8,128)(2,1)}, bf16[576,1024]{1,0:T(8,128)(2,1)}, u32[]{:S(2)}, u32[]{:S(2)}) collective-permute-start(bf16[576,1024]{1,0:T(8,128)(2,1)} %pad_maximum_fusion.2), channel_id=1, source_target_pairs={{0,2},{1,3},{2,0},{3,1},{4,6},{5,7},{6,4},{7,5},{8,10},{9,11},{10,... | collective-permute-start | bytes 3538952 | tf_op jit(solution)/shard_map/ppermute | solution.py:16
  53.4 54.1 %collective-permute-start.13 = (bf16[576,1024]{1,0:T(8,128)(2,1)}, bf16[576,1024]{1,0:T(8,128)(2,1)}, u32[]{:S(2)}, u32[]{:S(2)}) collective-permute-start(bf16[576,1024]{1,0:T(8,128)(2,1)} %pad_maximum_fusion.2), channel_id=1, source_target_pairs={{0,1},{1,0},{2,3},{3,2},{4,5},{5,4},{6,7},{7,6},{8,9},{9,8},{10,11... | collective-permute-start | bytes 3538952 | tf_op jit(solution)/shard_map/ppermute | solution.py:16
  62.7 42.4 %collective-permute-start.7 = (bf16[576,1024]{1,0:T(8,128)(2,1)}, bf16[576,1024]{1,0:T(8,128)(2,1)}, u32[]{:S(2)}, u32[]{:S(2)}) collective-permute-start(bf16[576,1024]{1,0:T(8,128)(2,1)} %pad_maximum_fusion.1), channel_id=1, source_target_pairs={{0,2},{1,3},{2,0},{3,1},{4,6},{5,7},{6,4},{7,5},{8,10},{9,11},{10,... | collective-permute-start | bytes 3538952 | tf_op jit(solution)/shard_map/ppermute | solution.py:16
  65.9 45.7 %collective-permute-start.6 = (bf16[576,1024]{1,0:T(8,128)(2,1)}, bf16[576,1024]{1,0:T(8,128)(2,1)}, u32[]{:S(2)}, u32[]{:S(2)}) collective-permute-start(bf16[576,1024]{1,0:T(8,128)(2,1)} %pad_maximum_fusion.1), channel_id=1, source_target_pairs={{0,1},{1,0},{2,3},{3,2},{4,5},{5,4},{6,7},{7,6},{8,9},{9,8},{10,11... | collective-permute-start | bytes 3538952 | tf_op jit(solution)/shard_map/ppermute | solution.py:16
  81.0 34.3 %collective-permute-start.15 = (bf16[576,1024]{1,0:T(8,128)(2,1)}, bf16[576,1024]{1,0:T(8,128)(2,1)S(1)}, u32[]{:S(2)}, u32[]{:S(2)}) collective-permute-start(bf16[576,1024]{1,0:T(8,128)(2,1)} %collective-permute-done.14), channel_id=1, source_target_pairs={{0,1},{1,0},{2,3},{3,2},{4,5},{5,4},{6,7},{7,6},{8,9},{9,8},{10,11... | collective-permute-start | bytes 3538952 | tf_op jit(solution)/shard_map/ppermute | solution.py:16
  136.1 52.7 %all-to-all-start.4 = ((bf16[8,32,4096]{2,1,0:T(8,128)(2,1)}), bf16[8,32,4096]{2,1,0:T(8,128)(2,1)}, u32[]{:S(2)}, u32[]{:S(2)}) async-start(bf16[8,32,4096]{2,1,0:T(8,128)(2,1)} %bitcast.133), calls=%async_computation.4 | async-start | bytes 4194304 | tf_op jit(solution)/shard_map/all_to_all | solution.py:78
  188.8 52.3 %all-to-all-start.2 = ((bf16[8,32,4096]{2,1,0:T(8,128)(2,1)}), bf16[8,32,4096]{2,1,0:T(8,128)(2,1)}, u32[]{:S(2)}, u32[]{:S(2)}) async-start(bf16[8,32,4096]{2,1,0:T(8,128)(2,1)} %bitcast.132), calls=%async_computation.2 | async-start | bytes 4194304 | tf_op jit(solution)/shard_map/all_to_all | solution.py:78
  254.6 52.4 %all-to-all-start.3 = ((bf16[8,32,4096]{2,1,0:T(8,128)(2,1)}), bf16[8,32,4096]{2,1,0:T(8,128)(2,1)}, u32[]{:S(2)}, u32[]{:S(2)}) async-start(bf16[8,32,4096]{2,1,0:T(8,128)(2,1)} %get-tuple-element.50), calls=%async_computation.3 | async-start | bytes 4194304 | tf_op jit(solution)/shard_map/all_to_all | solution.py:78
  262.6 56.0 %collective-permute-start.17 = (bf16[576,1024]{1,0:T(8,128)(2,1)}, bf16[576,1024]{1,0:T(8,128)(2,1)}, u32[]{:S(2)}, u32[]{:S(2)}) collective-permute-start(bf16[576,1024]{1,0:T(8,128)(2,1)} %convolution_convert_fusion), channel_id=1, source_target_pairs={{0,1},{1,0},{2,3},{3,2},{4,5},{5,4},{6,7},{7,6},{8,9},{9,8},{10,11... | collective-permute-start | bytes 3538952 | tf_op jit(solution)/shard_map/ppermute | solution.py:16
  264.0 48.8 %collective-permute-start.25 = (bf16[144,1024]{1,0:T(8,128)(2,1)}, bf16[144,1024]{1,0:T(8,128)(2,1)}, u32[]{:S(2)}, u32[]{:S(2)}) collective-permute-start(bf16[144,1024]{1,0:T(8,128)(2,1)} %get-tuple-element.23), channel_id=1, source_target_pairs={{0,12},{4,8},{8,4},{12,0},{16,28},{20,24},{24,20},{28,16},{1,13},{... | collective-permute-start | bytes 884744 | tf_op jit(solution)/shard_map/ppermute | solution.py:16
  266.9 45.8 %collective-permute-start.24 = (bf16[144,1024]{1,0:T(8,128)(2,1)}, bf16[144,1024]{1,0:T(8,128)(2,1)}, u32[]{:S(2)}, u32[]{:S(2)}) collective-permute-start(bf16[144,1024]{1,0:T(8,128)(2,1)} %get-tuple-element.24), channel_id=1, source_target_pairs={{0,8},{4,12},{8,0},{12,4},{16,24},{20,28},{24,16},{28,20},{1,9},{5... | collective-permute-start | bytes 884744 | tf_op jit(solution)/shard_map/ppermute | solution.py:16
  267.5 45.3 %collective-permute-start.23 = (bf16[144,1024]{1,0:T(8,128)(2,1)}, bf16[144,1024]{1,0:T(8,128)(2,1)}, u32[]{:S(2)}, u32[]{:S(2)}) collective-permute-start(bf16[144,1024]{1,0:T(8,128)(2,1)} %get-tuple-element.25), channel_id=1, source_target_pairs={{0,4},{4,0},{8,12},{12,8},{16,20},{20,16},{24,28},{28,24},{1,5},{5... | collective-permute-start | bytes 884744 | tf_op jit(solution)/shard_map/ppermute | solution.py:16
  307.0 95.1 %all-to-all-start.5 = ((bf16[8,32,4096]{2,1,0:T(8,128)(2,1)}), bf16[8,32,4096]{2,1,0:T(8,128)(2,1)}, u32[]{:S(2)}, u32[]{:S(2)}) async-start(bf16[8,32,4096]{2,1,0:T(8,128)(2,1)} %get-tuple-element.49), calls=%async_computation.5 | async-start | bytes 4194304 | tf_op jit(solution)/shard_map/all_to_all | solution.py:78
  315.2 29.2 %collective-permute-start.27 = (bf16[576,1024]{1,0:T(8,128)(2,1)}, bf16[576,1024]{1,0:T(8,128)(2,1)}, u32[]{:S(2)}, u32[]{:S(2)}) collective-permute-start(bf16[576,1024]{1,0:T(8,128)(2,1)} %pad_maximum_fusion.3), channel_id=1, source_target_pairs={{0,2},{1,3},{2,0},{3,1},{4,6},{5,7},{6,4},{7,5},{8,10},{9,11},{10,... | collective-permute-start | bytes 3538952 | tf_op jit(solution)/shard_map/ppermute | solution.py:16
  318.5 31.2 %collective-permute-start.16 = (bf16[576,1024]{1,0:T(8,128)(2,1)}, bf16[576,1024]{1,0:T(8,128)(2,1)}, u32[]{:S(2)}, u32[]{:S(2)}) collective-permute-start(bf16[576,1024]{1,0:T(8,128)(2,1)} %convolution_convert_fusion.2), channel_id=1, source_target_pairs={{0,1},{1,0},{2,3},{3,2},{4,5},{5,4},{6,7},{7,6},{8,9},{9,8},{10,11... | collective-permute-start | bytes 3538952 | tf_op jit(solution)/shard_map/ppermute | solution.py:16
  321.6 46.7 %collective-permute-start.18 = (bf16[576,1024]{1,0:T(8,128)(2,1)}, bf16[576,1024]{1,0:T(8,128)(2,1)}, u32[]{:S(2)}, u32[]{:S(2)}) collective-permute-start(bf16[576,1024]{1,0:T(8,128)(2,1)} %add_convert_fusion.1), channel_id=1, source_target_pairs={{0,2},{1,3},{2,0},{3,1},{4,6},{5,7},{6,4},{7,5},{8,10},{9,11},{10,... | collective-permute-start | bytes 3538952 | tf_op jit(solution)/shard_map/ppermute | solution.py:16
  322.2 66.9 %collective-permute-start.26 = (bf16[576,1024]{1,0:T(8,128)(2,1)}, bf16[576,1024]{1,0:T(8,128)(2,1)}, u32[]{:S(2)}, u32[]{:S(2)}) collective-permute-start(bf16[576,1024]{1,0:T(8,128)(2,1)} %pad_maximum_fusion.3), channel_id=1, source_target_pairs={{0,1},{1,0},{2,3},{3,2},{4,5},{5,4},{6,7},{7,6},{8,9},{9,8},{10,11... | collective-permute-start | bytes 3538952 | tf_op jit(solution)/shard_map/ppermute | solution.py:16
  344.3 30.1 %collective-permute-start.28 = (bf16[576,1024]{1,0:T(8,128)(2,1)}, bf16[576,1024]{1,0:T(8,128)(2,1)}, u32[]{:S(2)}, u32[]{:S(2)}) collective-permute-start(bf16[576,1024]{1,0:T(8,128)(2,1)} %collective-permute-done.27), channel_id=1, source_target_pairs={{0,1},{1,0},{2,3},{3,2},{4,5},{5,4},{6,7},{7,6},{8,9},{9,8},{10,11... | collective-permute-start | bytes 3538952 | tf_op jit(solution)/shard_map/ppermute | solution.py:16
  (30 other events, 258.1 us)
where the time goes:
time: 417 us; the launch traced here: 415 us
  waiting for transfers between devices  251 us (60%)
  starting transfers between devices  57.4 us (14%)
  matrix products  32 us (8%)
  other arithmetic  29.4 us (7%)
  local copies, waits for them, and re-layouts  22.8 us (5%)
  Pallas kernels  12.5 us (3%)
  between operations  9.1 us (2%)
    all_to_all x6, waiting for transfers between devices, spread(): lax.all_to_all(value, 'expert', split_axis=0, concat_axis=0, tiled=True)  132 us
    ppermute x29, waiting for transfers between devices, swap(): return lax.ppermute(value, axis, [(j, j ^ mask) for j in range(size)])  119 us
    dot_general x22, matrix products, dot(): lax.dot_general(left, right, (dims, ((), ())), preferred_element_type=jnp...  32 us
    ppermute x29, starting transfers between devices, swap(): return lax.ppermute(value, axis, [(j, j ^ mask) for j in range(size)])  30 us
    all_to_all x6, starting transfers between devices, spread(): lax.all_to_all(value, 'expert', split_axis=0, concat_axis=0, tiled=True)  27.4 us
    pallas_call x1, Pallas kernels, finish(): pl.pallas_call(finish_body, out_shape=(jax.ShapeDtypeStruct(shape, jnp.fl...  12.5 us
    gather x3, local copies, waits for them, and re-layouts, relocate(): pieces = jnp.take(pieces, source, axis=0)  9.42 us
  transfers between devices with their start and end apart: 35, of which 17 were waited for; matrix products, arithmetic and copies ran while one was open for 19% of the time, Pallas kernels for 0%

commit v1 on v0

--- a/solution.py
+++ b/solution.py
@@ -38,7 +38,8 @@
     return parts[0]
 
 
-def finish_body(lane_ref, grad_ref, first_ref, second_ref, out_first, out_second, out_step):
+def finish_body(lane_ref, grad_ref, first_ref, second_ref, *refs):
+    out_first, out_second, out_step = refs[-3:]
     weight_grad = grad_ref[0]
     new_first = beta_one * first_ref[...].astype(jnp.float32) + (1.0 - beta_one) * weight_grad
     scaled = (1.0 - beta_two) * weight_grad * weight_grad
@@ -48,30 +49,30 @@
     out_step[...] = (new_first / (jnp.sqrt(new_second) + epsilon)).astype(jnp.bfloat16)
 
 
-def finish(lane, weight_grad, first, second):
+def finish(part, lane, weight_grad, moments, earlier):
     ways, hidden, columns = weight_grad.shape
     rows = max(hidden // 4, 16)
-    wide = pl.BlockSpec((rows, columns), lambda k, i, lane: (i, lane[0] ^ k))
-    shape = (hidden, ways * columns)
+    few = ways // 2
+    out = pl.BlockSpec((rows, columns), lambda d, i, lane: (i, part * few + d))
+    kinds = (jnp.float32, jnp.float32, jnp.bfloat16)
     return pl.pallas_call(
         finish_body,
-        out_shape=(
-            jax.ShapeDtypeStruct(shape, jnp.float32),
-            jax.ShapeDtypeStruct(shape, jnp.float32),
-            jax.ShapeDtypeStruct(shape, jnp.bfloat16),
-        ),
+        out_shape=tuple(jax.ShapeDtypeStruct((hidden, ways * columns), kind) for kind in kinds),
         grid_spec=pltpu.PrefetchScalarGridSpec(
             num_scalar_prefetch=1,
-            grid=(ways, hidden // rows),
+            grid=(few, hidden // rows),
             in_specs=[
-                pl.BlockSpec((1, rows, columns), lambda k, i, lane: (k, i, 0)),
-                wide,
-                wide,
-            ],
-            out_specs=(wide, wide, wide),
+                pl.BlockSpec(
+                    (1, rows, columns), lambda d, i, lane: (lane[0] ^ (part * few + d), i, 0)
+                ),
+                pl.BlockSpec((rows, columns), lambda d, i, lane: (i, d)),
+                pl.BlockSpec((rows, columns), lambda d, i, lane: (i, few + d)),
+            ]
+            + [pl.BlockSpec(memory_space=pl.ANY)] * len(earlier),
+            out_specs=(out, out, out),
         ),
-        name="finish",
-    )(lane.reshape(1), weight_grad, first, second)
+        input_output_aliases={4 + k: k for k in range(len(earlier))},
+    )(lane.reshape(1), weight_grad, moments, moments, *earlier)
 
 
 def spread(value):
@@ -80,6 +81,10 @@
 
 def dot(left, right, dims):
     return lax.dot_general(left, right, (dims, ((), ())), preferred_element_type=jnp.float32)
+
+
+ROWS = ((0,), (0,))
+COLUMNS = ((1,), (1,))
 
 
 def per_device(
@@ -106,29 +111,38 @@
     place = lax.axis_index("expert")
     side = place // half
     lane = lax.axis_index("dp")
-    spot = (place % half) ^ jnp.arange(half, dtype=jnp.int32)
 
     homes = jnp.arange(devices, dtype=jnp.int32)
     matched = (next_home[:, None] == homes[None, :]).astype(jnp.int32)
     source = jnp.sum(matched * previous_home[:, None], axis=0)
 
+    def pick(stack, index):
+        return jnp.take(stack, index, axis=0, mode="clip")
+
     def relocate(value):
         rows = value.shape[0] // devices
         pieces = spread(value.reshape(devices, rows, value.shape[1]))
-        pieces = jnp.take(pieces, source, axis=0)
+        pieces = pick(pieces, source)
         return spread(pieces).reshape(value.shape)
 
     def across_half(blocks):
-        moved = [blocks[r] if r == 0 else swap(blocks[r], "expert", r) for r in range(half)]
-        return jnp.concatenate(moved, axis=0)
-
-    far_tokens = swap(tokens, "expert", half)
-    far_routes = swap(routes, "expert", half)
-    far_gates = swap(gate_weights, "expert", half)
-    far_grads = swap(out_grad, "expert", half)
-
-    old_first = relocate(first_moment[0].astype(jnp.bfloat16))
-    old_second = relocate(second_moment[0].astype(jnp.bfloat16))
+        return [blocks[r] if r == 0 else swap(blocks[r], "expert", r) for r in range(half)]
+
+    def cross(value):
+        return swap(value, "expert", half)
+
+    far_routes = cross(routes)
+    far_gates = cross(gate_weights)
+    far_tokens = cross(tokens)
+    far_grads = cross(out_grad)
+
+    middle = w_out.shape[2] // 2
+    packed = []
+    for cut in (slice(0, middle), slice(middle, None)):
+        pieces = (first_moment[0][:, cut], second_moment[0][:, cut])
+        packed.append(jnp.concatenate(pieces, axis=1).astype(jnp.bfloat16))
+    old_first = relocate(packed[0])
+    old_second = relocate(packed[1])
 
     both_routes = jnp.stack([routes, far_routes])
     both_gates = jnp.stack([gate_weights, far_gates])
@@ -164,7 +178,8 @@
     plain = ((1,), (0,))
 
     def deliver(rows):
-        rows = send(rows)
+        blocks = send(rows)
+        rows = jnp.concatenate(blocks, axis=0)
         return gather_parts(rows, "dp")
 
     rows_parts = deliver(dot(picks_now, both_tokens, plain))
@@ -172,7 +187,8 @@
     next_parts = deliver(dot(picks_next, both_grads, plain) * gate_next)
 
     order = lane ^ jnp.arange(ways, dtype=jnp.int32)
-    weight_in = jnp.concatenate([w_in[0, 0], w_in[0, 1]], axis=1).reshape(ways, columns, 2 * hidden)
+    weight_in = jnp.concatenate([w_in[0, 0], w_in[0, 1]], axis=1)
+    weight_in = weight_in.reshape(ways, columns, 2 * hidden)
     weight_out = w_out[0].reshape(hidden, ways, columns)
     weight_in = [lax.dynamic_index_in_dim(weight_in, order[k], 0, False) for k in range(ways)]
     weight_out = [lax.dynamic_index_in_dim(weight_out, order[k], 1, False) for k in range(ways)]
@@ -181,24 +197,42 @@
     gate_pre, up_value = pre[:, :hidden], pre[:, hidden:]
     sigmoid_gate = jax.nn.sigmoid(gate_pre)
     silu_gate = gate_pre * sigmoid_gate
-    activation = (silu_gate * up_value).astype(jnp.bfloat16).reshape(half, 2 * capacity, hidden)
-    activation = jnp.take(activation, spot, axis=0).reshape(slots, hidden)
-    activation = relocate(activation)
-    activation = jnp.take(activation.reshape(half, 2 * capacity, hidden), spot, axis=0)
-    activation = activation.reshape(slots, hidden)
-    act_grad = sum(dot(grad_parts[k], weight_out[k], ((1,), (1,))) for k in range(ways))
+    activation = (silu_gate * up_value).astype(jnp.bfloat16)
+    activation, gate_pre, up_value = lax.optimization_barrier((activation, gate_pre, up_value))
+    sigmoid_gate = jax.nn.sigmoid(gate_pre)
+    silu_gate = gate_pre * sigmoid_gate
+    held, mask, places = activation[None], half, [0]
+    while mask > 1:
+        held = jnp.concatenate([held, swap(held, "expert", mask)], axis=0)
+        places += [k ^ mask for k in places]
+        mask //= 2
+    places = jnp.array(places, jnp.int32)
+
+    def holder(target):
+        wanted = source[target] ^ place
+        return jnp.sum(jnp.where(places == wanted & -2, jnp.arange(half, dtype=jnp.int32), 0))
+
+    other = swap(pick(held, holder(place ^ 1)), "expert", 1)
+    shift = source[place] ^ place
+    activation = jnp.where(shift & 1 == 1, other, pick(held, holder(place)))
+    numbers = jnp.arange(devices, dtype=jnp.int32)
+    numbers = 2 * ((numbers // 2) ^ (shift % half)) + (numbers & 1)
+    activation = activation.reshape(devices, capacity, hidden)
+    activation = pick(activation, numbers).reshape(slots, hidden)
+    act_grad = sum(dot(grad_parts[k], weight_out[k], COLUMNS) for k in range(ways))
     gate_grad = act_grad * up_value * sigmoid_gate * (1.0 + gate_pre * (1.0 - sigmoid_gate))
     up_grad = act_grad * silu_gate
     both_grad = jnp.concatenate([gate_grad, up_grad], axis=1).astype(jnp.bfloat16)
-    pieces = [dot(both_grad, weight_in[k], ((1,), (1,))).astype(jnp.bfloat16) for k in range(ways)]
+    pieces = [dot(both_grad, w, COLUMNS).astype(jnp.bfloat16) for w in weight_in]
     summed = scatter_sum(pieces, "dp").astype(jnp.bfloat16)
-    returned = across_half(summed.reshape(half, 2 * capacity, columns))
+    returned = jnp.concatenate(across_half(summed.reshape(half, 2 * capacity, columns)), axis=0)
     token_sums = dot(picks_now, returned, ((0,), (0,)))
-    far_sums = swap(token_sums[tok_count:].astype(jnp.bfloat16), "expert", half)
+    far_sums = cross(token_sums[tok_count:].astype(jnp.bfloat16))
     token_grad = (token_sums[:tok_count] + far_sums.astype(jnp.float32)).astype(jnp.bfloat16)
 
-    weight_grad = jnp.stack([dot(activation, part, ((0,), (0,))) for part in next_parts])
-    new_first, new_second, adam_step = finish(lane, weight_grad, old_first, old_second)
+    weight_grad = jnp.stack([dot(activation, part, ROWS) for part in next_parts])
+    begun = finish(0, lane, weight_grad, old_first, ())
+    new_first, new_second, adam_step = finish(1, lane, weight_grad, old_second, begun)
     return (token_grad, new_first[None], new_second[None], adam_step[None])
 
 

time: 417 us -> 369 us (0.88)
  waiting for transfers between devices: 251 us -> 196 us
  starting transfers between devices: 57.4 us -> 62.6 us
  other arithmetic: 29.4 us -> 24.8 us
    all_to_all x6 -> x4, waiting for transfers between devices: 132 us -> 23.6 us  [spread(): lax.all_to_all(value, 'expert', split_axis=0, concat_axis=0, tiled=True)]
    ppermute x29 -> x32, waiting for transfers between devices: 119 us -> 172 us  [swap(): return lax.ppermute(value, axis, [(j, j ^ mask) for j in range(size)])]
    ppermute x29 -> x32, starting transfers between devices: 30 us -> 40.3 us  [swap(): return lax.ppermute(value, axis, [(j, j ^ mask) for j in range(size)])]
    convert_element_type x2 -> x0, other arithmetic: 7.59 us -> none  [the longest x1 3.79 us: per_device(): old_second = relocate(second_moment[0].astype(jnp.bfloat16))]
    concatenate x3 -> x7, other arithmetic: 4.72 us -> 11.9 us  [the longest x3 4.61 us: deliver(): rows = jnp.concatenate(blocks, axis=0)]
    select_n x7 -> x1, other arithmetic: 8.32 us -> 1.74 us  [per_device(): activation = jnp.where(shift & 1 == 1, other, pick(held, holder(place)))]
    all_to_all x6 -> x4, starting transfers between devices: 27.4 us -> 22.3 us  [spread(): lax.all_to_all(value, 'expert', split_axis=0, concat_axis=0, tiled=True)]
    gather x5 -> x4, local copies, waits for them, and re-layouts: 13.3 us -> 8.43 us  [pick(): return jnp.take(stack, index, axis=0, mode='clip')]
  transfers between devices with their start and end apart: 35 -> 36, of which waited for: 17 -> 15; matrix products, arithmetic and copies ran while one was open for 19% -> 20% of each run, Pallas kernels for 0% -> 2%
where the time goes in v1:
time: 369 us; the launch traced here: 367 us
  waiting for transfers between devices  196 us (53%)
  starting transfers between devices  62.6 us (17%)
  matrix products  33.9 us (9%)
  local copies, waits for them, and re-layouts  25.6 us (7%)
  other arithmetic  24.8 us (7%)
  Pallas kernels  14 us (4%)
  between operations  10.2 us (3%)
    ppermute x32, waiting for transfers between devices, swap(): return lax.ppermute(value, axis, [(j, j ^ mask) for j in range(size)])  172 us
    ppermute x32, starting transfers between devices, swap(): return lax.ppermute(value, axis, [(j, j ^ mask) for j in range(size)])  40.3 us
    dot_general x22, matrix products, dot(): lax.dot_general(left, right, (dims, ((), ())), preferred_element_type=jnp...  33.9 us
    all_to_all x4, waiting for transfers between devices, spread(): lax.all_to_all(value, 'expert', split_axis=0, concat_axis=0, tiled=True)  23.6 us
    all_to_all x4, starting transfers between devices, spread(): lax.all_to_all(value, 'expert', split_axis=0, concat_axis=0, tiled=True)  22.3 us
    pallas_call x2, Pallas kernels, finish(): pl.pallas_call(finish_body, out_shape=tuple((jax.ShapeDtypeStruct((hidden...  14 us
    unnamed x68, local copies, waits for them, and re-layouts  10.5 us
    gather x4, local copies, waits for them, and re-layouts, pick(): return jnp.take(stack, index, axis=0, mode='clip')  8.43 us
  transfers between devices with their start and end apart: 36, of which 15 were waited for; matrix products, arithmetic and copies ran while one was open for 20% of the time, Pallas kernels for 2%

profile of v1, /device:TPU:0, one launch (start us, length us, event | category | flops | bytes accessed | tf_op | source)
XLA Modules:
  0.0 367.0 jit_solution(8516011145985267949)
XLA Ops:
  8.2 7.4 %all-to-all-start.2 = ((bf16[8,32,4096]{2,1,0:T(8,128)(2,1)}), bf16[8,32,4096]{2,1,0:T(8,128)(2,1)S(1)}, u32[]{:S(2)}, u32[]{:S(2)}) async-start(bf16[8,32,4096]{2,1,0:T(8,128)(2,1)} %pad_maximum_fusion.2), calls=%async_computation.2 | async-start | bytes 4194304 | tf_op jit(solution)/shard_map/all_to_all | solution.py:79
  26.3 50.3 %collective-permute-done = s32[128,4]{0,1:T(4,128)S(1)} collective-permute-done((s32[128,4]{0,1:T(4,128)S(1)}, s32[128,4]{0,1:T(4,128)S(1)}, u32[]{:S(2)}, u32[]{:S(2)}) %collective-permute-start) | collective-permute-done | bytes 2080 | tf_op jit(solution)/shard_map/ppermute | solution.py:16
  78.7 4.4 %all-to-all-start = ((bf16[8,32,4096]{2,1,0:T(8,128)(2,1)}), bf16[8,32,4096]{2,1,0:T(8,128)(2,1)}, u32[]{:S(2)}, u32[]{:S(2)}) async-start(bf16[8,32,4096]{2,1,0:T(8,128)(2,1)} %pad_maximum_fusion.1), calls=%async_computation | async-start | bytes 4194304 | tf_op jit(solution)/shard_map/all_to_all | solution.py:79
  91.3 6.7 %collective-permute-start.5 = (bf16[144,1024]{1,0:T(8,128)(2,1)S(1)}, bf16[144,1024]{1,0:T(8,128)(2,1)S(1)}, u32[]{:S(2)}, u32[]{:S(2)}) collective-permute-start(bf16[144,1024]{1,0:T(8,128)(2,1)S(1)} %get-tuple-element.76), channel_id=1, source_target_pairs={{0,12},{4,8},{8,4},{12,0},{16,28},{20,24},{24,20},{28,16},{1,13},{... | collective-permute-start | bytes 884744 | tf_op jit(solution)/shard_map/ppermute | solution.py:16
  98.0 26.3 %collective-permute-done.12 = bf16[144,1024]{1,0:T(8,128)(2,1)S(1)} collective-permute-done((bf16[144,1024]{1,0:T(8,128)(2,1)S(1)}, bf16[144,1024]{1,0:T(8,128)(2,1)S(1)}, u32[]{:S(2)}, u32[]{:S(2)}) %collective-permute-start.12) | collective-permute-done | bytes 294944 | tf_op jit(solution)/shard_map/ppermute | solution.py:16
  126.2 7.4 %collective-permute-done.11 = bf16[144,1024]{1,0:T(8,128)(2,1)S(1)} collective-permute-done((bf16[144,1024]{1,0:T(8,128)(2,1)S(1)}, bf16[144,1024]{1,0:T(8,128)(2,1)S(1)}, u32[]{:S(2)}, u32[]{:S(2)}) %collective-permute-start.11) | collective-permute-done | bytes 294944 | tf_op jit(solution)/shard_map/ppermute | solution.py:16
  136.3 5.1 %collective-permute-done.5 = bf16[144,1024]{1,0:T(8,128)(2,1)S(1)} collective-permute-done((bf16[144,1024]{1,0:T(8,128)(2,1)S(1)}, bf16[144,1024]{1,0:T(8,128)(2,1)S(1)}, u32[]{:S(2)}, u32[]{:S(2)}) %collective-permute-start.5) | collective-permute-done | bytes 294944 | tf_op jit(solution)/shard_map/ppermute | solution.py:16
  141.4 4.1 %collective-permute-done.4 = bf16[144,1024]{1,0:T(8,128)(2,1)S(1)} collective-permute-done((bf16[144,1024]{1,0:T(8,128)(2,1)S(1)}, bf16[144,1024]{1,0:T(8,128)(2,1)S(1)}, u32[]{:S(2)}, u32[]{:S(2)}) %collective-permute-start.4) | collective-permute-done | bytes 294944 | tf_op jit(solution)/shard_map/ppermute | solution.py:16
  155.7 4.1 %copy.29 = bf16[1,256,4096]{1,2,0:T(8,128)(2,1)} copy(bf16[1,256,4096]{2,1,0:T(8,128)(2,1)} %param.18) | data formatting | bytes 4194304 | tf_op args[7]
  164.0 22.9 %collective-permute-done.7 = bf16[576,1024]{1,0:T(8,128)(2,1)} collective-permute-done((bf16[576,1024]{1,0:T(8,128)(2,1)}, bf16[576,1024]{1,0:T(8,128)(2,1)}, u32[]{:S(2)}, u32[]{:S(2)}) %collective-permute-start.7) | collective-permute-done | bytes 1179680 | tf_op jit(solution)/shard_map/ppermute | solution.py:16
  186.8 3.6 gather_fusion.2
  190.4 4.5 %all-to-all-start.3 = ((bf16[8,32,4096]{2,1,0:T(8,128)(2,1)}), bf16[8,32,4096]{2,1,0:T(8,128)(2,1)}, u32[]{:S(2)}, u32[]{:S(2)}) async-start(bf16[8,32,4096]{2,1,0:T(8,128)(2,1)} %gather_fusion.2), calls=%async_computation.3 | async-start | bytes 4194304 | tf_op jit(solution)/shard_map/all_to_all | solution.py:79
  217.3 3.6 gather_fusion.1
  221.0 23.6 %all-to-all-done.3 = bf16[8,32,4096]{2,1,0:T(8,128)(2,1)} async-done(((bf16[8,32,4096]{2,1,0:T(8,128)(2,1)}), bf16[8,32,4096]{2,1,0:T(8,128)(2,1)}, u32[]{:S(2)}, u32[]{:S(2)}) %all-to-all-start.3) | async-done | bytes 2097184 | tf_op jit(solution)/shard_map/all_to_all | solution.py:79
  244.6 6.0 %all-to-all-start.1 = ((bf16[8,32,4096]{2,1,0:T(8,128)(2,1)}), bf16[8,32,4096]{2,1,0:T(8,128)(2,1)}, u32[]{:S(2)}, u32[]{:S(2)}) async-start(bf16[8,32,4096]{2,1,0:T(8,128)(2,1)} %gather_fusion.1), calls=%async_computation.1 | async-start | bytes 4194304 | tf_op jit(solution)/shard_map/all_to_all | solution.py:79
  259.1 4.6 %collective-permute-start.24 = (bf16[2,576,256]{2,1,0:T(8,128)(2,1)}, bf16[2,576,256]{2,1,0:T(8,128)(2,1)}, u32[]{:S(2)}, u32[]{:S(2)}) collective-permute-start(bf16[2,576,256]{2,1,0:T(8,128)(2,1)} %pad_maximum_fusion.8), channel_id=1, source_target_pairs={{0,8},{4,12},{8,0},{12,4},{16,24},{20,28},{24,16},{28,20},{1,9},{5... | collective-permute-start | bytes 1769480 | tf_op jit(solution)/shard_map/ppermute | solution.py:16
  267.9 3.1 add_convert_fusion.1
  273.9 29.2 %collective-permute-done.24 = bf16[2,576,256]{2,1,0:T(8,128)(2,1)} collective-permute-done((bf16[2,576,256]{2,1,0:T(8,128)(2,1)}, bf16[2,576,256]{2,1,0:T(8,128)(2,1)}, u32[]{:S(2)}, u32[]{:S(2)}) %collective-permute-start.24) | collective-permute-done | bytes 589856 | tf_op jit(solution)/shard_map/ppermute | solution.py:16
  309.6 5.5 %collective-permute-done.25 = bf16[576,256]{1,0:T(8,128)(2,1)} collective-permute-done((bf16[576,256]{1,0:T(8,128)(2,1)S(1)}, bf16[576,256]{1,0:T(8,128)(2,1)}, u32[]{:S(2)}, u32[]{:S(2)}) %collective-permute-start.25) | collective-permute-done | bytes 294944 | tf_op jit(solution)/shard_map/ppermute | solution.py:16
  329.0 3.7 %collective-permute-done.21 = bf16[144,1024]{1,0:T(8,128)(2,1)S(1)} collective-permute-done((bf16[144,1024]{1,0:T(8,128)(2,1)S(1)}, bf16[144,1024]{1,0:T(8,128)(2,1)S(1)}, u32[]{:S(2)}, u32[]{:S(2)}) %collective-permute-start.21) | collective-permute-done | bytes 294944 | tf_op jit(solution)/shard_map/ppermute | solution.py:16
  332.7 3.6 collective-permute-done.20
  342.4 9.8 %collective-permute-done.22 = bf16[128,1024]{1,0:T(8,128)(2,1)S(1)} collective-permute-done((bf16[128,1024]{1,0:T(8,128)(2,1)S(1)}, bf16[128,1024]{1,0:T(8,128)(2,1)S(1)}, u32[]{:S(2)}, u32[]{:S(2)}) %collective-permute-start.22) | collective-permute-done | bytes 262176 | tf_op jit(solution)/shard_map/ppermute | solution.py:16
  353.0 7.0 %shard_map.138 = (f32[256,4096]{1,0:T(8,128)}, f32[256,4096]{1,0:T(8,128)}, bf16[256,4096]{1,0:T(8,128)(2,1)}) custom-call(s32[1]{0:T(128)} %bitcast.27.lane_ref, f32[4,256,1024]{2,1,0:T(8,128)} %pad_maximum_fusion.grad_ref, bf16[256,4096]{1,0:T(8,128)(2,1)} %bitcast.52.first_ref.second_ref, bf16[256,4096]{1,0:T(8,128)(2,1)} %bitcast.52.first_ref.second_ref), custom_call_target="tpu_custom_call" | custom-call | tf_op jit(solution)/shard_map/pallas_call | solution.py:58
  360.0 7.0 %shard_map.139 = (f32[256,4096]{1,0:T(8,128)}, f32[256,4096]{1,0:T(8,128)}, bf16[256,4096]{1,0:T(8,128)(2,1)}) custom-call(s32[1]{0:T(128)} %bitcast.27.lane_ref, f32[4,256,1024]{2,1,0:T(8,128)} %pad_maximum_fusion.grad_ref, bf16[256,4096]{1,0:T(8,128)(2,1)} %bitcast.49.first_ref.second_ref, ...), custom_call_target="tpu_custom_call", output_to_operand_aliasing={{0}: (4, {}), {1}: (5, {}), {2}: (6, {})} | custom-call | tf_op jit(solution)/shard_map/pallas_call | solution.py:58
  (196 shorter events, 103.4 us)
Async XLA Ops:
  8.2 69.1 %all-to-all-start.2 = ((bf16[8,32,4096]{2,1,0:T(8,128)(2,1)}), bf16[8,32,4096]{2,1,0:T(8,128)(2,1)S(1)}, u32[]{:S(2)}, u32[]{:S(2)}) async-start(bf16[8,32,4096]{2,1,0:T(8,128)(2,1)} %pad_maximum_fusion.2), calls=%async_computation.2 | async-start | bytes 4194304 | tf_op jit(solution)/shard_map/all_to_all | solution.py:79
  15.6 61.0 %collective-permute-start = (s32[128,4]{0,1:T(4,128)S(1)}, s32[128,4]{0,1:T(4,128)S(1)}, u32[]{:S(2)}, u32[]{:S(2)}) collective-permute-start(s32[128,4]{0,1:T(4,128)S(1)} %copy-done.28), channel_id=1, source_target_pairs={{0,16},{4,20},{8,24},{12,28},{16,0},{20,4},{24,8},{28,12},{1,17},{... | collective-permute-start | bytes 6152 | tf_op jit(solution)/shard_map/ppermute | solution.py:16
  18.5 58.1 %collective-permute-start.2 = (f32[128,4]{0,1:T(4,128)S(1)}, f32[128,4]{0,1:T(4,128)S(1)}, u32[]{:S(2)}, u32[]{:S(2)}) collective-permute-start(f32[128,4]{0,1:T(4,128)S(1)} %copy-done.29), channel_id=1, source_target_pairs={{0,16},{4,20},{8,24},{12,28},{16,0},{20,4},{24,8},{28,12},{1,17},{... | collective-permute-start | bytes 6152 | tf_op jit(solution)/shard_map/ppermute | solution.py:16
  18.6 65.7 %collective-permute-start.9 = (bf16[128,1024]{1,0:T(8,128)(2,1)}, bf16[128,1024]{1,0:T(8,128)(2,1)}, u32[]{:S(2)}, u32[]{:S(2)}) collective-permute-start(bf16[128,1024]{1,0:T(8,128)(2,1)} %param.11), channel_id=1, source_target_pairs={{0,16},{4,20},{8,24},{12,28},{16,0},{20,4},{24,8},{28,12},{1,17},{... | collective-permute-start | bytes 786440 | tf_op jit(solution)/shard_map/ppermute | solution.py:16
  21.5 68.0 %collective-permute-start.1 = (bf16[128,1024]{1,0:T(8,128)(2,1)}, bf16[128,1024]{1,0:T(8,128)(2,1)}, u32[]{:S(2)}, u32[]{:S(2)}) collective-permute-start(bf16[128,1024]{1,0:T(8,128)(2,1)} %param.12), channel_id=1, source_target_pairs={{0,16},{4,20},{8,24},{12,28},{16,0},{20,4},{24,8},{28,12},{1,17},{... | collective-permute-start | bytes 786440 | tf_op jit(solution)/shard_map/ppermute | solution.py:16
  78.7 111.7 %all-to-all-start = ((bf16[8,32,4096]{2,1,0:T(8,128)(2,1)}), bf16[8,32,4096]{2,1,0:T(8,128)(2,1)}, u32[]{:S(2)}, u32[]{:S(2)}) async-start(bf16[8,32,4096]{2,1,0:T(8,128)(2,1)} %pad_maximum_fusion.1), calls=%async_computation | async-start | bytes 4194304 | tf_op jit(solution)/shard_map/all_to_all | solution.py:79
  86.0 38.3 %collective-permute-start.12 = (bf16[144,1024]{1,0:T(8,128)(2,1)S(1)}, bf16[144,1024]{1,0:T(8,128)(2,1)S(1)}, u32[]{:S(2)}, u32[]{:S(2)}) collective-permute-start(bf16[144,1024]{1,0:T(8,128)(2,1)S(1)} %get-tuple-element.72), channel_id=1, source_target_pairs={{0,12},{4,8},{8,4},{12,0},{16,28},{20,24},{24,20},{28,16},{1,13},{... | collective-permute-start | bytes 884744 | tf_op jit(solution)/shard_map/ppermute | solution.py:16
  88.8 44.9 %collective-permute-start.11 = (bf16[144,1024]{1,0:T(8,128)(2,1)S(1)}, bf16[144,1024]{1,0:T(8,128)(2,1)S(1)}, u32[]{:S(2)}, u32[]{:S(2)}) collective-permute-start(bf16[144,1024]{1,0:T(8,128)(2,1)S(1)} %get-tuple-element.73), channel_id=1, source_target_pairs={{0,8},{4,12},{8,0},{12,4},{16,24},{20,28},{24,16},{28,20},{1,9},{5... | collective-permute-start | bytes 884744 | tf_op jit(solution)/shard_map/ppermute | solution.py:16
  89.4 44.3 %collective-permute-start.10 = (bf16[144,1024]{1,0:T(8,128)(2,1)S(1)}, bf16[144,1024]{1,0:T(8,128)(2,1)S(1)}, u32[]{:S(2)}, u32[]{:S(2)}) collective-permute-start(bf16[144,1024]{1,0:T(8,128)(2,1)S(1)} %get-tuple-element.74), channel_id=1, source_target_pairs={{0,4},{4,0},{8,12},{12,8},{16,20},{20,16},{24,28},{28,24},{1,5},{5... | collective-permute-start | bytes 884744 | tf_op jit(solution)/shard_map/ppermute | solution.py:16
  91.3 50.1 %collective-permute-start.5 = (bf16[144,1024]{1,0:T(8,128)(2,1)S(1)}, bf16[144,1024]{1,0:T(8,128)(2,1)S(1)}, u32[]{:S(2)}, u32[]{:S(2)}) collective-permute-start(bf16[144,1024]{1,0:T(8,128)(2,1)S(1)} %get-tuple-element.76), channel_id=1, source_target_pairs={{0,12},{4,8},{8,4},{12,0},{16,28},{20,24},{24,20},{28,16},{1,13},{... | collective-permute-start | bytes 884744 | tf_op jit(solution)/shard_map/ppermute | solution.py:16
  98.0 47.6 %collective-permute-start.4 = (bf16[144,1024]{1,0:T(8,128)(2,1)S(1)}, bf16[144,1024]{1,0:T(8,128)(2,1)S(1)}, u32[]{:S(2)}, u32[]{:S(2)}) collective-permute-start(bf16[144,1024]{1,0:T(8,128)(2,1)S(1)} %get-tuple-element.77), channel_id=1, source_target_pairs={{0,8},{4,12},{8,0},{12,4},{16,24},{20,28},{24,16},{28,20},{1,9},{5... | collective-permute-start | bytes 884744 | tf_op jit(solution)/shard_map/ppermute | solution.py:16
  146.8 40.0 %collective-permute-start.7 = (bf16[576,1024]{1,0:T(8,128)(2,1)}, bf16[576,1024]{1,0:T(8,128)(2,1)}, u32[]{:S(2)}, u32[]{:S(2)}) collective-permute-start(bf16[576,1024]{1,0:T(8,128)(2,1)} %pad_maximum_fusion.3), channel_id=1, source_target_pairs={{0,2},{1,3},{2,0},{3,1},{4,6},{5,7},{6,4},{7,5},{8,10},{9,11},{10,... | collective-permute-start | bytes 3538952 | tf_op jit(solution)/shard_map/ppermute | solution.py:16
  150.0 49.4 %collective-permute-start.6 = (bf16[576,1024]{1,0:T(8,128)(2,1)}, bf16[576,1024]{1,0:T(8,128)(2,1)}, u32[]{:S(2)}, u32[]{:S(2)}) collective-permute-start(bf16[576,1024]{1,0:T(8,128)(2,1)} %pad_maximum_fusion.3), channel_id=1, source_target_pairs={{0,1},{1,0},{2,3},{3,2},{4,5},{5,4},{6,7},{7,6},{8,9},{9,8},{10,11... | collective-permute-start | bytes 3538952 | tf_op jit(solution)/shard_map/ppermute | solution.py:16
  162.3 39.4 %collective-permute-start.13 = (bf16[576,1024]{1,0:T(8,128)(2,1)}, bf16[576,1024]{1,0:T(8,128)(2,1)}, u32[]{:S(2)}, u32[]{:S(2)}) collective-permute-start(bf16[576,1024]{1,0:T(8,128)(2,1)} %pad_maximum_fusion.4), channel_id=1, source_target_pairs={{0,1},{1,0},{2,3},{3,2},{4,5},{5,4},{6,7},{7,6},{8,9},{9,8},{10,11... | collective-permute-start | bytes 3538952 | tf_op jit(solution)/shard_map/ppermute | solution.py:16
  164.0 40.8 %collective-permute-start.15 = (bf16[576,1024]{1,0:T(8,128)(2,1)}, bf16[576,1024]{1,0:T(8,128)(2,1)S(1)}, u32[]{:S(2)}, u32[]{:S(2)}) collective-permute-start(bf16[576,1024]{1,0:T(8,128)(2,1)} %collective-permute-done.14), channel_id=1, source_target_pairs={{0,1},{1,0},{2,3},{3,2},{4,5},{5,4},{6,7},{7,6},{8,9},{9,8},{10,11... | collective-permute-start | bytes 3538952 | tf_op jit(solution)/shard_map/ppermute | solution.py:16
  190.4 54.2 %all-to-all-start.3 = ((bf16[8,32,4096]{2,1,0:T(8,128)(2,1)}), bf16[8,32,4096]{2,1,0:T(8,128)(2,1)}, u32[]{:S(2)}, u32[]{:S(2)}) async-start(bf16[8,32,4096]{2,1,0:T(8,128)(2,1)} %gather_fusion.2), calls=%async_computation.3 | async-start | bytes 4194304 | tf_op jit(solution)/shard_map/all_to_all | solution.py:79
  209.5 58.4 %collective-permute-start.17 = (bf16[576,1024]{1,0:T(8,128)(2,1)}, bf16[576,1024]{1,0:T(8,128)(2,1)}, u32[]{:S(2)}, u32[]{:S(2)}) collective-permute-start(bf16[576,1024]{1,0:T(8,128)(2,1)} %convolution_convert_fusion), channel_id=1, source_target_pairs={{0,1},{1,0},{2,3},{3,2},{4,5},{5,4},{6,7},{7,6},{8,9},{9,8},{10,11... | collective-permute-start | bytes 3538952 | tf_op jit(solution)/shard_map/ppermute | solution.py:16
  211.5 39.1 %collective-permute-start.28 = (bf16[144,1024]{1,0:T(8,128)(2,1)}, bf16[144,1024]{1,0:T(8,128)(2,1)}, u32[]{:S(2)}, u32[]{:S(2)}) collective-permute-start(bf16[144,1024]{1,0:T(8,128)(2,1)} %get-tuple-element.59), channel_id=1, source_target_pairs={{0,12},{4,8},{8,4},{12,0},{16,28},{20,24},{24,20},{28,16},{1,13},{... | collective-permute-start | bytes 884744 | tf_op jit(solution)/shard_map/ppermute | solution.py:16
  215.0 42.2 %collective-permute-start.23 = (bf16[1,576,256]{2,1,0:T(8,128)(2,1)S(1)}, bf16[1,576,256]{2,1,0:T(8,128)(2,1)}, u32[]{:S(2)}, u32[]{:S(2)}) collective-permute-start(bf16[1,576,256]{2,1,0:T(8,128)(2,1)S(1)} %bitcast.155), channel_id=1, source_target_pairs={{0,16},{4,20},{8,24},{12,28},{16,0},{20,4},{24,8},{28,12},{1,17},{... | collective-permute-start | bytes 884744 | tf_op jit(solution)/shard_map/ppermute | solution.py:16
  244.6 115.4 %all-to-all-start.1 = ((bf16[8,32,4096]{2,1,0:T(8,128)(2,1)}), bf16[8,32,4096]{2,1,0:T(8,128)(2,1)}, u32[]{:S(2)}, u32[]{:S(2)}) async-start(bf16[8,32,4096]{2,1,0:T(8,128)(2,1)} %gather_fusion.1), calls=%async_computation.1 | async-start | bytes 4194304 | tf_op jit(solution)/shard_map/all_to_all | solution.py:79
  252.9 53.3 %collective-permute-start.30 = (bf16[576,1024]{1,0:T(8,128)(2,1)}, bf16[576,1024]{1,0:T(8,128)(2,1)}, u32[]{:S(2)}, u32[]{:S(2)}) collective-permute-start(bf16[576,1024]{1,0:T(8,128)(2,1)} %pad_maximum_fusion.6), channel_id=1, source_target_pairs={{0,2},{1,3},{2,0},{3,1},{4,6},{5,7},{6,4},{7,5},{8,10},{9,11},{10,... | collective-permute-start | bytes 3538952 | tf_op jit(solution)/shard_map/ppermute | solution.py:16
  259.1 44.0 %collective-permute-start.24 = (bf16[2,576,256]{2,1,0:T(8,128)(2,1)}, bf16[2,576,256]{2,1,0:T(8,128)(2,1)}, u32[]{:S(2)}, u32[]{:S(2)}) collective-permute-start(bf16[2,576,256]{2,1,0:T(8,128)(2,1)} %pad_maximum_fusion.8), channel_id=1, source_target_pairs={{0,8},{4,12},{8,0},{12,4},{16,24},{20,28},{24,16},{28,20},{1,9},{5... | collective-permute-start | bytes 1769480 | tf_op jit(solution)/shard_map/ppermute | solution.py:16
  267.9 51.4 %collective-permute-start.16 = (bf16[576,1024]{1,0:T(8,128)(2,1)}, bf16[576,1024]{1,0:T(8,128)(2,1)}, u32[]{:S(2)}, u32[]{:S(2)}) collective-permute-start(bf16[576,1024]{1,0:T(8,128)(2,1)} %convolution_convert_fusion.2), channel_id=1, source_target_pairs={{0,1},{1,0},{2,3},{3,2},{4,5},{5,4},{6,7},{7,6},{8,9},{9,8},{10,11... | collective-permute-start | bytes 3538952 | tf_op jit(solution)/shard_map/ppermute | solution.py:16
  271.0 48.3 %collective-permute-start.18 = (bf16[576,1024]{1,0:T(8,128)(2,1)}, bf16[576,1024]{1,0:T(8,128)(2,1)}, u32[]{:S(2)}, u32[]{:S(2)}) collective-permute-start(bf16[576,1024]{1,0:T(8,128)(2,1)} %add_convert_fusion.1), channel_id=1, source_target_pairs={{0,2},{1,3},{2,0},{3,1},{4,6},{5,7},{6,4},{7,5},{8,10},{9,11},{10,... | collective-permute-start | bytes 3538952 | tf_op jit(solution)/shard_map/ppermute | solution.py:16
  (45 other events, 528.3 us)

commit v2 on v1

--- a/solution.py
+++ b/solution.py
@@ -189,9 +189,11 @@
     order = lane ^ jnp.arange(ways, dtype=jnp.int32)
     weight_in = jnp.concatenate([w_in[0, 0], w_in[0, 1]], axis=1)
     weight_in = weight_in.reshape(ways, columns, 2 * hidden)
-    weight_out = w_out[0].reshape(hidden, ways, columns)
     weight_in = [lax.dynamic_index_in_dim(weight_in, order[k], 0, False) for k in range(ways)]
-    weight_out = [lax.dynamic_index_in_dim(weight_out, order[k], 1, False) for k in range(ways)]
+    weight_out = [
+        lax.dynamic_slice(w_out[0], (0, order[k] * columns), (hidden, columns))
+        for k in range(ways)
+    ]
 
     pre = sum(dot(rows_parts[k], weight_in[k], plain) for k in range(ways))
     gate_pre, up_value = pre[:, :hidden], pre[:, hidden:]

time: 369 us -> 371 us (level)
    unnamed x68 -> x75, local copies, waits for them, and re-layouts: 10.5 us -> 5.98 us
  transfers between devices with their start and end apart: 36 -> 36, of which waited for: 15 -> 16; matrix products, arithmetic and copies ran while one was open for 20% -> 19% of each run, Pallas kernels for 2% -> 2%
where the time goes in v2:
time: 371 us; the launch traced here: 369 us
  waiting for transfers between devices  196 us (53%)
  starting transfers between devices  64.3 us (17%)
  matrix products  33.8 us (9%)
  other arithmetic  25.1 us (7%)
  local copies, waits for them, and re-layouts  22.7 us (6%)
  Pallas kernels  14.1 us (4%)
  between operations  13.1 us (4%)
    ppermute x32, waiting for transfers between devices, swap(): return lax.ppermute(value, axis, [(j, j ^ mask) for j in range(size)])  173 us
    ppermute x32, starting transfers between devices, swap(): return lax.ppermute(value, axis, [(j, j ^ mask) for j in range(size)])  42 us
    dot_general x22, matrix products, dot(): lax.dot_general(left, right, (dims, ((), ())), preferred_element_type=jnp...  33.8 us
    all_to_all x4, waiting for transfers between devices, spread(): lax.all_to_all(value, 'expert', split_axis=0, concat_axis=0, tiled=True)  22.7 us
    all_to_all x4, starting transfers between devices, spread(): lax.all_to_all(value, 'expert', split_axis=0, concat_axis=0, tiled=True)  22.3 us
    pallas_call x2, Pallas kernels, finish(): pl.pallas_call(finish_body, out_shape=tuple((jax.ShapeDtypeStruct((hidden...  14.1 us
    gather x4, local copies, waits for them, and re-layouts, pick(): return jnp.take(stack, index, axis=0, mode='clip')  9.22 us
  transfers between devices with their start and end apart: 36, of which 16 were waited for; matrix products, arithmetic and copies ran while one was open for 19% of the time, Pallas kernels for 2%

profile of v2, /device:TPU:0, one launch (start us, length us, event | category | flops | bytes accessed | tf_op | source)
XLA Modules:
  0.0 369.1 jit_solution(11087520190256098792)
XLA Ops:
  8.4 7.4 %all-to-all-start.2 = ((bf16[8,32,4096]{2,1,0:T(8,128)(2,1)}), bf16[8,32,4096]{2,1,0:T(8,128)(2,1)}, u32[]{:S(2)}, u32[]{:S(2)}) async-start(bf16[8,32,4096]{2,1,0:T(8,128)(2,1)} %pad_maximum_fusion.2), calls=%async_computation.2 | async-start | bytes 4194304 | tf_op jit(solution)/shard_map/all_to_all | solution.py:79
  26.5 50.4 %collective-permute-done = s32[128,4]{0,1:T(4,128)S(1)} collective-permute-done((s32[128,4]{0,1:T(4,128)S(1)}, s32[128,4]{0,1:T(4,128)S(1)}, u32[]{:S(2)}, u32[]{:S(2)}) %collective-permute-start) | collective-permute-done | bytes 2080 | tf_op jit(solution)/shard_map/ppermute | solution.py:16
  77.5 4.4 %all-to-all-start = ((bf16[8,32,4096]{2,1,0:T(8,128)(2,1)}), bf16[8,32,4096]{2,1,0:T(8,128)(2,1)}, u32[]{:S(2)}, u32[]{:S(2)}) async-start(bf16[8,32,4096]{2,1,0:T(8,128)(2,1)} %pad_maximum_fusion.1), calls=%async_computation | async-start | bytes 4194304 | tf_op jit(solution)/shard_map/all_to_all | solution.py:79
  91.3 8.6 %collective-permute-start.5 = (bf16[144,1024]{1,0:T(8,128)(2,1)S(1)}, bf16[144,1024]{1,0:T(8,128)(2,1)S(1)}, u32[]{:S(2)}, u32[]{:S(2)}) collective-permute-start(bf16[144,1024]{1,0:T(8,128)(2,1)S(1)} %get-tuple-element.76), channel_id=1, source_target_pairs={{0,12},{4,8},{8,4},{12,0},{16,28},{20,24},{24,20},{28,16},{1,13},{... | collective-permute-start | bytes 884744 | tf_op jit(solution)/shard_map/ppermute | solution.py:16
  99.9 23.3 %collective-permute-done.12 = bf16[144,1024]{1,0:T(8,128)(2,1)S(1)} collective-permute-done((bf16[144,1024]{1,0:T(8,128)(2,1)S(1)}, bf16[144,1024]{1,0:T(8,128)(2,1)S(1)}, u32[]{:S(2)}, u32[]{:S(2)}) %collective-permute-start.12) | collective-permute-done | bytes 294944 | tf_op jit(solution)/shard_map/ppermute | solution.py:16
  125.1 8.1 %collective-permute-done.11 = bf16[144,1024]{1,0:T(8,128)(2,1)S(1)} collective-permute-done((bf16[144,1024]{1,0:T(8,128)(2,1)S(1)}, bf16[144,1024]{1,0:T(8,128)(2,1)S(1)}, u32[]{:S(2)}, u32[]{:S(2)}) %collective-permute-start.11) | collective-permute-done | bytes 294944 | tf_op jit(solution)/shard_map/ppermute | solution.py:16
  135.8 5.7 %collective-permute-done.5 = bf16[144,1024]{1,0:T(8,128)(2,1)S(1)} collective-permute-done((bf16[144,1024]{1,0:T(8,128)(2,1)S(1)}, bf16[144,1024]{1,0:T(8,128)(2,1)S(1)}, u32[]{:S(2)}, u32[]{:S(2)}) %collective-permute-start.5) | collective-permute-done | bytes 294944 | tf_op jit(solution)/shard_map/ppermute | solution.py:16
  141.5 4.2 %collective-permute-done.4 = bf16[144,1024]{1,0:T(8,128)(2,1)S(1)} collective-permute-done((bf16[144,1024]{1,0:T(8,128)(2,1)S(1)}, bf16[144,1024]{1,0:T(8,128)(2,1)S(1)}, u32[]{:S(2)}, u32[]{:S(2)}) %collective-permute-start.4) | collective-permute-done | bytes 294944 | tf_op jit(solution)/shard_map/ppermute | solution.py:16
  163.4 24.2 %collective-permute-done.7 = bf16[576,1024]{1,0:T(8,128)(2,1)} collective-permute-done((bf16[576,1024]{1,0:T(8,128)(2,1)}, bf16[576,1024]{1,0:T(8,128)(2,1)}, u32[]{:S(2)}, u32[]{:S(2)}) %collective-permute-start.7) | collective-permute-done | bytes 1179680 | tf_op jit(solution)/shard_map/ppermute | solution.py:16
  187.6 3.6 gather_fusion.2
  191.3 4.5 %all-to-all-start.3 = ((bf16[8,32,4096]{2,1,0:T(8,128)(2,1)}), bf16[8,32,4096]{2,1,0:T(8,128)(2,1)}, u32[]{:S(2)}, u32[]{:S(2)}) async-start(bf16[8,32,4096]{2,1,0:T(8,128)(2,1)} %gather_fusion.2), calls=%async_computation.3 | async-start | bytes 4194304 | tf_op jit(solution)/shard_map/all_to_all | solution.py:79
  219.1 3.6 gather_fusion.1
  222.7 22.7 %all-to-all-done.3 = bf16[8,32,4096]{2,1,0:T(8,128)(2,1)} async-done(((bf16[8,32,4096]{2,1,0:T(8,128)(2,1)}), bf16[8,32,4096]{2,1,0:T(8,128)(2,1)}, u32[]{:S(2)}, u32[]{:S(2)}) %all-to-all-start.3) | async-done | bytes 2097184 | tf_op jit(solution)/shard_map/all_to_all | solution.py:79
  245.4 6.0 %all-to-all-start.1 = ((bf16[8,32,4096]{2,1,0:T(8,128)(2,1)}), bf16[8,32,4096]{2,1,0:T(8,128)(2,1)}, u32[]{:S(2)}, u32[]{:S(2)}) async-start(bf16[8,32,4096]{2,1,0:T(8,128)(2,1)} %gather_fusion.1), calls=%async_computation.1 | async-start | bytes 4194304 | tf_op jit(solution)/shard_map/all_to_all | solution.py:79
  259.9 4.6 %collective-permute-start.24 = (bf16[2,576,256]{2,1,0:T(8,128)(2,1)}, bf16[2,576,256]{2,1,0:T(8,128)(2,1)}, u32[]{:S(2)}, u32[]{:S(2)}) collective-permute-start(bf16[2,576,256]{2,1,0:T(8,128)(2,1)} %pad_maximum_fusion.8), channel_id=1, source_target_pairs={{0,8},{4,12},{8,0},{12,4},{16,24},{20,28},{24,16},{28,20},{1,9},{5... | collective-permute-start | bytes 1769480 | tf_op jit(solution)/shard_map/ppermute | solution.py:16
  265.9 3.0 convolution_convert_fusion.2
  268.9 3.1 add_convert_fusion.1
  274.8 29.1 %collective-permute-done.24 = bf16[2,576,256]{2,1,0:T(8,128)(2,1)} collective-permute-done((bf16[2,576,256]{2,1,0:T(8,128)(2,1)}, bf16[2,576,256]{2,1,0:T(8,128)(2,1)}, u32[]{:S(2)}, u32[]{:S(2)}) %collective-permute-start.24) | collective-permute-done | bytes 589856 | tf_op jit(solution)/shard_map/ppermute | solution.py:16
  311.1 5.8 %collective-permute-done.25 = bf16[576,256]{1,0:T(8,128)(2,1)} collective-permute-done((bf16[576,256]{1,0:T(8,128)(2,1)}, bf16[576,256]{1,0:T(8,128)(2,1)}, u32[]{:S(2)}, u32[]{:S(2)}) %collective-permute-start.25) | collective-permute-done | bytes 294944 | tf_op jit(solution)/shard_map/ppermute | solution.py:16
  330.8 3.7 %collective-permute-done.21 = bf16[144,1024]{1,0:T(8,128)(2,1)S(1)} collective-permute-done((bf16[144,1024]{1,0:T(8,128)(2,1)S(1)}, bf16[144,1024]{1,0:T(8,128)(2,1)S(1)}, u32[]{:S(2)}, u32[]{:S(2)}) %collective-permute-start.21) | collective-permute-done | bytes 294944 | tf_op jit(solution)/shard_map/ppermute | solution.py:16
  334.5 3.6 collective-permute-done.20
  344.3 9.8 %collective-permute-done.22 = bf16[128,1024]{1,0:T(8,128)(2,1)S(1)} collective-permute-done((bf16[128,1024]{1,0:T(8,128)(2,1)S(1)}, bf16[128,1024]{1,0:T(8,128)(2,1)S(1)}, u32[]{:S(2)}, u32[]{:S(2)}) %collective-permute-start.22) | collective-permute-done | bytes 262176 | tf_op jit(solution)/shard_map/ppermute | solution.py:16
  354.8 7.0 %shard_map.138 = (f32[256,4096]{1,0:T(8,128)}, f32[256,4096]{1,0:T(8,128)}, bf16[256,4096]{1,0:T(8,128)(2,1)}) custom-call(s32[1]{0:T(128)} %bitcast.26.lane_ref, f32[4,256,1024]{2,1,0:T(8,128)} %pad_maximum_fusion.grad_ref, bf16[256,4096]{1,0:T(8,128)(2,1)} %bitcast.51.first_ref.second_ref, bf16[256,4096]{1,0:T(8,128)(2,1)} %bitcast.51.first_ref.second_ref), custom_call_target="tpu_custom_call" | custom-call | tf_op jit(solution)/shard_map/pallas_call | solution.py:58
  361.8 7.1 %shard_map.139 = (f32[256,4096]{1,0:T(8,128)}, f32[256,4096]{1,0:T(8,128)}, bf16[256,4096]{1,0:T(8,128)(2,1)}) custom-call(s32[1]{0:T(128)} %bitcast.26.lane_ref, f32[4,256,1024]{2,1,0:T(8,128)} %pad_maximum_fusion.grad_ref, bf16[256,4096]{1,0:T(8,128)(2,1)} %bitcast.48.first_ref.second_ref, ...), custom_call_target="tpu_custom_call", output_to_operand_aliasing={{0}: (4, {}), {1}: (5, {}), {2}: (6, {})} | custom-call | tf_op jit(solution)/shard_map/pallas_call | solution.py:58
  (203 shorter events, 102.5 us)
Async XLA Ops:
  8.4 69.1 %all-to-all-start.2 = ((bf16[8,32,4096]{2,1,0:T(8,128)(2,1)}), bf16[8,32,4096]{2,1,0:T(8,128)(2,1)}, u32[]{:S(2)}, u32[]{:S(2)}) async-start(bf16[8,32,4096]{2,1,0:T(8,128)(2,1)} %pad_maximum_fusion.2), calls=%async_computation.2 | async-start | bytes 4194304 | tf_op jit(solution)/shard_map/all_to_all | solution.py:79
  15.8 61.0 %collective-permute-start = (s32[128,4]{0,1:T(4,128)S(1)}, s32[128,4]{0,1:T(4,128)S(1)}, u32[]{:S(2)}, u32[]{:S(2)}) collective-permute-start(s32[128,4]{0,1:T(4,128)S(1)} %copy-done.32), channel_id=1, source_target_pairs={{0,16},{4,20},{8,24},{12,28},{16,0},{20,4},{24,8},{28,12},{1,17},{... | collective-permute-start | bytes 6152 | tf_op jit(solution)/shard_map/ppermute | solution.py:16
  18.7 58.1 %collective-permute-start.2 = (f32[128,4]{0,1:T(4,128)S(1)}, f32[128,4]{0,1:T(4,128)S(1)}, u32[]{:S(2)}, u32[]{:S(2)}) collective-permute-start(f32[128,4]{0,1:T(4,128)S(1)} %copy-done.33), channel_id=1, source_target_pairs={{0,16},{4,20},{8,24},{12,28},{16,0},{20,4},{24,8},{28,12},{1,17},{... | collective-permute-start | bytes 6152 | tf_op jit(solution)/shard_map/ppermute | solution.py:16
  18.8 64.3 %collective-permute-start.9 = (bf16[128,1024]{1,0:T(8,128)(2,1)}, bf16[128,1024]{1,0:T(8,128)(2,1)}, u32[]{:S(2)}, u32[]{:S(2)}) collective-permute-start(bf16[128,1024]{1,0:T(8,128)(2,1)} %param.11), channel_id=1, source_target_pairs={{0,16},{4,20},{8,24},{12,28},{16,0},{20,4},{24,8},{28,12},{1,17},{... | collective-permute-start | bytes 786440 | tf_op jit(solution)/shard_map/ppermute | solution.py:16
  21.6 67.9 %collective-permute-start.1 = (bf16[128,1024]{1,0:T(8,128)(2,1)}, bf16[128,1024]{1,0:T(8,128)(2,1)}, u32[]{:S(2)}, u32[]{:S(2)}) collective-permute-start(bf16[128,1024]{1,0:T(8,128)(2,1)} %param.12), channel_id=1, source_target_pairs={{0,16},{4,20},{8,24},{12,28},{16,0},{20,4},{24,8},{28,12},{1,17},{... | collective-permute-start | bytes 786440 | tf_op jit(solution)/shard_map/ppermute | solution.py:16
  77.5 113.8 %all-to-all-start = ((bf16[8,32,4096]{2,1,0:T(8,128)(2,1)}), bf16[8,32,4096]{2,1,0:T(8,128)(2,1)}, u32[]{:S(2)}, u32[]{:S(2)}) async-start(bf16[8,32,4096]{2,1,0:T(8,128)(2,1)} %pad_maximum_fusion.1), calls=%async_computation | async-start | bytes 4194304 | tf_op jit(solution)/shard_map/all_to_all | solution.py:79
  84.8 38.5 %collective-permute-start.12 = (bf16[144,1024]{1,0:T(8,128)(2,1)S(1)}, bf16[144,1024]{1,0:T(8,128)(2,1)S(1)}, u32[]{:S(2)}, u32[]{:S(2)}) collective-permute-start(bf16[144,1024]{1,0:T(8,128)(2,1)S(1)} %get-tuple-element.72), channel_id=1, source_target_pairs={{0,12},{4,8},{8,4},{12,0},{16,28},{20,24},{24,20},{28,16},{1,13},{... | collective-permute-start | bytes 884744 | tf_op jit(solution)/shard_map/ppermute | solution.py:16
  87.6 45.5 %collective-permute-start.11 = (bf16[144,1024]{1,0:T(8,128)(2,1)S(1)}, bf16[144,1024]{1,0:T(8,128)(2,1)S(1)}, u32[]{:S(2)}, u32[]{:S(2)}) collective-permute-start(bf16[144,1024]{1,0:T(8,128)(2,1)S(1)} %get-tuple-element.73), channel_id=1, source_target_pairs={{0,8},{4,12},{8,0},{12,4},{16,24},{20,28},{24,16},{28,20},{1,9},{5... | collective-permute-start | bytes 884744 | tf_op jit(solution)/shard_map/ppermute | solution.py:16
  88.2 45.0 %collective-permute-start.10 = (bf16[144,1024]{1,0:T(8,128)(2,1)S(1)}, bf16[144,1024]{1,0:T(8,128)(2,1)S(1)}, u32[]{:S(2)}, u32[]{:S(2)}) collective-permute-start(bf16[144,1024]{1,0:T(8,128)(2,1)S(1)} %get-tuple-element.74), channel_id=1, source_target_pairs={{0,4},{4,0},{8,12},{12,8},{16,20},{20,16},{24,28},{28,24},{1,5},{5... | collective-permute-start | bytes 884744 | tf_op jit(solution)/shard_map/ppermute | solution.py:16
  91.3 50.2 %collective-permute-start.5 = (bf16[144,1024]{1,0:T(8,128)(2,1)S(1)}, bf16[144,1024]{1,0:T(8,128)(2,1)S(1)}, u32[]{:S(2)}, u32[]{:S(2)}) collective-permute-start(bf16[144,1024]{1,0:T(8,128)(2,1)S(1)} %get-tuple-element.76), channel_id=1, source_target_pairs={{0,12},{4,8},{8,4},{12,0},{16,28},{20,24},{24,20},{28,16},{1,13},{... | collective-permute-start | bytes 884744 | tf_op jit(solution)/shard_map/ppermute | solution.py:16
  99.9 45.8 %collective-permute-start.4 = (bf16[144,1024]{1,0:T(8,128)(2,1)S(1)}, bf16[144,1024]{1,0:T(8,128)(2,1)S(1)}, u32[]{:S(2)}, u32[]{:S(2)}) collective-permute-start(bf16[144,1024]{1,0:T(8,128)(2,1)S(1)} %get-tuple-element.77), channel_id=1, source_target_pairs={{0,8},{4,12},{8,0},{12,4},{16,24},{20,28},{24,16},{28,20},{1,9},{5... | collective-permute-start | bytes 884744 | tf_op jit(solution)/shard_map/ppermute | solution.py:16
  146.9 40.7 %collective-permute-start.7 = (bf16[576,1024]{1,0:T(8,128)(2,1)}, bf16[576,1024]{1,0:T(8,128)(2,1)}, u32[]{:S(2)}, u32[]{:S(2)}) collective-permute-start(bf16[576,1024]{1,0:T(8,128)(2,1)} %pad_maximum_fusion.3), channel_id=1, source_target_pairs={{0,2},{1,3},{2,0},{3,1},{4,6},{5,7},{6,4},{7,5},{8,10},{9,11},{10,... | collective-permute-start | bytes 3538952 | tf_op jit(solution)/shard_map/ppermute | solution.py:16
  150.8 49.3 %collective-permute-start.6 = (bf16[576,1024]{1,0:T(8,128)(2,1)}, bf16[576,1024]{1,0:T(8,128)(2,1)}, u32[]{:S(2)}, u32[]{:S(2)}) collective-permute-start(bf16[576,1024]{1,0:T(8,128)(2,1)} %pad_maximum_fusion.3), channel_id=1, source_target_pairs={{0,1},{1,0},{2,3},{3,2},{4,5},{5,4},{6,7},{7,6},{8,9},{9,8},{10,11... | collective-permute-start | bytes 3538952 | tf_op jit(solution)/shard_map/ppermute | solution.py:16
  161.8 40.7 %collective-permute-start.13 = (bf16[576,1024]{1,0:T(8,128)(2,1)}, bf16[576,1024]{1,0:T(8,128)(2,1)}, u32[]{:S(2)}, u32[]{:S(2)}) collective-permute-start(bf16[576,1024]{1,0:T(8,128)(2,1)} %pad_maximum_fusion.4), channel_id=1, source_target_pairs={{0,1},{1,0},{2,3},{3,2},{4,5},{5,4},{6,7},{7,6},{8,9},{9,8},{10,11... | collective-permute-start | bytes 3538952 | tf_op jit(solution)/shard_map/ppermute | solution.py:16
  163.4 43.0 %collective-permute-start.15 = (bf16[576,1024]{1,0:T(8,128)(2,1)}, bf16[576,1024]{1,0:T(8,128)(2,1)S(1)}, u32[]{:S(2)}, u32[]{:S(2)}) collective-permute-start(bf16[576,1024]{1,0:T(8,128)(2,1)} %collective-permute-done.14), channel_id=1, source_target_pairs={{0,1},{1,0},{2,3},{3,2},{4,5},{5,4},{6,7},{7,6},{8,9},{9,8},{10,11... | collective-permute-start | bytes 3538952 | tf_op jit(solution)/shard_map/ppermute | solution.py:16
  191.3 54.1 %all-to-all-start.3 = ((bf16[8,32,4096]{2,1,0:T(8,128)(2,1)}), bf16[8,32,4096]{2,1,0:T(8,128)(2,1)}, u32[]{:S(2)}, u32[]{:S(2)}) async-start(bf16[8,32,4096]{2,1,0:T(8,128)(2,1)} %gather_fusion.2), calls=%async_computation.3 | async-start | bytes 4194304 | tf_op jit(solution)/shard_map/all_to_all | solution.py:79
  211.3 57.6 %collective-permute-start.17 = (bf16[576,1024]{1,0:T(8,128)(2,1)}, bf16[576,1024]{1,0:T(8,128)(2,1)}, u32[]{:S(2)}, u32[]{:S(2)}) collective-permute-start(bf16[576,1024]{1,0:T(8,128)(2,1)} %convolution_convert_fusion), channel_id=1, source_target_pairs={{0,1},{1,0},{2,3},{3,2},{4,5},{5,4},{6,7},{7,6},{8,9},{9,8},{10,11... | collective-permute-start | bytes 3538952 | tf_op jit(solution)/shard_map/ppermute | solution.py:16
  213.3 38.2 %collective-permute-start.28 = (bf16[144,1024]{1,0:T(8,128)(2,1)}, bf16[144,1024]{1,0:T(8,128)(2,1)}, u32[]{:S(2)}, u32[]{:S(2)}) collective-permute-start(bf16[144,1024]{1,0:T(8,128)(2,1)} %get-tuple-element.59), channel_id=1, source_target_pairs={{0,12},{4,8},{8,4},{12,0},{16,28},{20,24},{24,20},{28,16},{1,13},{... | collective-permute-start | bytes 884744 | tf_op jit(solution)/shard_map/ppermute | solution.py:16
  216.8 41.3 %collective-permute-start.23 = (bf16[1,576,256]{2,1,0:T(8,128)(2,1)S(1)}, bf16[1,576,256]{2,1,0:T(8,128)(2,1)}, u32[]{:S(2)}, u32[]{:S(2)}) collective-permute-start(bf16[1,576,256]{2,1,0:T(8,128)(2,1)S(1)} %bitcast.146), channel_id=1, source_target_pairs={{0,16},{4,20},{8,24},{12,28},{16,0},{20,4},{24,8},{28,12},{1,17},{... | collective-permute-start | bytes 884744 | tf_op jit(solution)/shard_map/ppermute | solution.py:16
  245.4 116.4 %all-to-all-start.1 = ((bf16[8,32,4096]{2,1,0:T(8,128)(2,1)}), bf16[8,32,4096]{2,1,0:T(8,128)(2,1)}, u32[]{:S(2)}, u32[]{:S(2)}) async-start(bf16[8,32,4096]{2,1,0:T(8,128)(2,1)} %gather_fusion.1), calls=%async_computation.1 | async-start | bytes 4194304 | tf_op jit(solution)/shard_map/all_to_all | solution.py:79
  253.9 53.8 %collective-permute-start.30 = (bf16[576,1024]{1,0:T(8,128)(2,1)}, bf16[576,1024]{1,0:T(8,128)(2,1)}, u32[]{:S(2)}, u32[]{:S(2)}) collective-permute-start(bf16[576,1024]{1,0:T(8,128)(2,1)} %pad_maximum_fusion.6), channel_id=1, source_target_pairs={{0,2},{1,3},{2,0},{3,1},{4,6},{5,7},{6,4},{7,5},{8,10},{9,11},{10,... | collective-permute-start | bytes 3538952 | tf_op jit(solution)/shard_map/ppermute | solution.py:16
  259.9 44.0 %collective-permute-start.24 = (bf16[2,576,256]{2,1,0:T(8,128)(2,1)}, bf16[2,576,256]{2,1,0:T(8,128)(2,1)}, u32[]{:S(2)}, u32[]{:S(2)}) collective-permute-start(bf16[2,576,256]{2,1,0:T(8,128)(2,1)} %pad_maximum_fusion.8), channel_id=1, source_target_pairs={{0,8},{4,12},{8,0},{12,4},{16,24},{20,28},{24,16},{28,20},{1,9},{5... | collective-permute-start | bytes 1769480 | tf_op jit(solution)/shard_map/ppermute | solution.py:16
  268.9 52.2 %collective-permute-start.16 = (bf16[576,1024]{1,0:T(8,128)(2,1)}, bf16[576,1024]{1,0:T(8,128)(2,1)}, u32[]{:S(2)}, u32[]{:S(2)}) collective-permute-start(bf16[576,1024]{1,0:T(8,128)(2,1)} %convolution_convert_fusion.2), channel_id=1, source_target_pairs={{0,1},{1,0},{2,3},{3,2},{4,5},{5,4},{6,7},{7,6},{8,9},{9,8},{10,11... | collective-permute-start | bytes 3538952 | tf_op jit(solution)/shard_map/ppermute | solution.py:16
  272.0 49.1 %collective-permute-start.18 = (bf16[576,1024]{1,0:T(8,128)(2,1)}, bf16[576,1024]{1,0:T(8,128)(2,1)}, u32[]{:S(2)}, u32[]{:S(2)}) collective-permute-start(bf16[576,1024]{1,0:T(8,128)(2,1)} %add_convert_fusion.1), channel_id=1, source_target_pairs={{0,2},{1,3},{2,0},{3,1},{4,6},{5,7},{6,4},{7,5},{8,10},{9,11},{10,... | collective-permute-start | bytes 3538952 | tf_op jit(solution)/shard_map/ppermute | solution.py:16
  (49 other events, 795.7 us)
